TPU v7x, 32 devices: a whole 2x2x4 slice. The times are simulated.
32 devices in a mesh: grp: 2 (over y), pos: 16 (over z, x, core).
Axes of the slice: x: 2, y: 2, z: 4, core: 2. Of those that a mesh axis runs over, the one named last changes fastest.
Arguments:
- object_field: float32 [2, 2048, 2048], P(None, 'grp', 'pos'), may hold values from -5 to 5
- probe_field: float32 [2, 256, 256], replicated, may hold values from -5 to 5
- patterns: float32 [96, 256, 256], P(('grp', 'pos')), may hold values from 0.05 to 5
- corners: int32 [2, 96], P(None, ('grp', 'pos')), may hold values from 0 to 1792, as said below
- counts: int32 [32], replicated, may hold values from 1 to 3, as said below
Outputs:
- object_new: float32 [2, 2048, 2048], P(None, 'grp', 'pos')
- probe_new: float32 [2, 256, 256], replicated
Inputs may be any that keep to these rules, and one draw needn't show every extreme that they name: `corners`: each slot's patch of 256 x 256 cells lies inside the object and inside its device's block of 1024 x 128 object cells extended by 128 cells on every side (the device at grp index a and pos index b holds rows a * 1024 to a * 1024 + 1023 and columns b * 128 to b * 128 + 127). The live slots of a device are its first counts[d] slots; some device has all 3 slots live.
All inputs are finite; a program needn't handle non-finite values.
Results may differ from a plain program's by a relative error of at most 0.00012.
Values sent between devices are 32-bit elements; how exact they have to be, the bound alone decides.
A program may use at most 64 MiB of HBM per device.

v0:
```python
import functools

import jax
import jax.numpy as jnp
import numpy as np
from jax import lax
from jax.experimental import pallas as pl
from jax.experimental.pallas import tpu as pltpu
from jax.sharding import PartitionSpec as P

HALO = 128
STEP_OBJECT = 0.25
STEP_PROBE = 4.0
MESH = pl.DeviceIdType.MESH


def dft_tables(order):
    indices = np.arange(order, dtype=np.int64)
    angles = (indices[:, None] * indices[None, :] % order) * (2.0 * np.pi / order)
    cos = np.cos(angles) / np.sqrt(order)
    sin = -np.sin(angles) / np.sqrt(order)
    left = np.block([[cos, -sin], [sin, cos]])
    right = np.block([[cos, sin], [-sin, cos]])
    both = np.stack([left, right]).astype(np.float32)
    high = both.astype(jnp.bfloat16)
    low = (both - high.astype(np.float32)).astype(jnp.bfloat16)
    return np.stack([high, low], axis=1)


def split(x):
    high = x.astype(jnp.bfloat16)
    low = (x - high.astype(jnp.float32)).astype(jnp.bfloat16)
    return high, low


def dot(a, b):
    return jnp.dot(a, b, preferred_element_type=jnp.float32)


def table_left(tab, which, data):
    high, low = split(data)
    th, tl = tab[which, 0], tab[which, 1]
    return dot(th, high) + (dot(th, low) + dot(tl, high))


def table_right(data, tab, which):
    high, low = split(data)
    th, tl = tab[which, 0], tab[which, 1]
    return dot(high, th) + (dot(low, th) + dot(high, tl))


def kernel(sizes, corners, counts, obj_hbm, prb_hbm, pat_hbm, tab_hbm, obj_out, prb_out,
           ext, prb, pat, tab, nb, stage, corv, cor_recv, cor_smem,
           gmid, gsend, grecv, gacc, yrecv, gp, p1r, p1, p2r, p2, p3r, pnew,
           loc, yh, corsem, cors, patsem, gsem, ysem, csem, gysem, asem, agsem, gasem, casem):
    G, PN, S, TR, M = sizes
    grp, pos = lax.axis_index("grp"), lax.axis_index("pos")
    core, chip, chips = lax.rem(pos, 2), pos // 2, PN // 2
    half = M // 2
    h2 = half // G
    h3 = max(8, h2 // chips)
    owners = h2 // h3

    def at(g, p):
        return {"device_id": (g, p), "device_id_type": MESH}

    col_peer = [at(grp, lax.rem(pos + PN - 1, PN)), at(grp, lax.rem(pos + 1, PN))]
    row_peer = [at(lax.rem(grp + G - 1, G), pos), at(lax.rem(grp + 1, G), pos)]
    col_send, col_recv = [pos > 0, pos < PN - 1], [pos < PN - 1, pos > 0]
    row_send, row_recv = [grp > 0, grp < G - 1], [grp < G - 1, grp > 0]
    partner = at(grp, pos + 1 - 2 * core)

    def grp_at(k):
        return lax.rem(grp + k, G)

    def chip_at(k):
        return lax.rem(chip + k, chips)

    locals_ = [
        pltpu.make_async_copy(obj_hbm, ext.at[:, pl.ds(HALO, TR), :], loc.at[0]),
        pltpu.make_async_copy(prb_hbm, prb, loc.at[1]),
        pltpu.make_async_copy(pat_hbm, pat, loc.at[2]),
        pltpu.make_async_copy(tab_hbm, tab, loc.at[3]),
    ]
    for c in locals_:
        c.start()

    barrier = pltpu.get_barrier_semaphore()
    for d in range(2):
        @pl.when(col_send[d])
        def _():
            pl.semaphore_signal(barrier, inc=1, **col_peer[d])
    for k in range(1, G):
        pl.semaphore_signal(barrier, inc=1, **at(grp_at(k), pos))
    for k in range(1, chips):
        pl.semaphore_signal(barrier, inc=1, **at(grp, chip_at(k) * 2 + core))
    pl.semaphore_signal(barrier, inc=1, **partner)
    expected = (pos > 0).astype(jnp.int32) + (pos < PN - 1).astype(jnp.int32) + G + chips - 1

    lane = lax.broadcasted_iota(jnp.int32, (M, HALO), 1)
    row8 = lax.broadcasted_iota(jnp.int32, (8, 128), 0)
    packed = jnp.zeros((8, 128), jnp.int32)
    for s in range(S):
        packed = jnp.where(row8 == s, corners[0, s] - grp * TR + HALO, packed)
    corv[...] = packed
    zero = jnp.zeros((HALO, HALO), jnp.float32)
    for s in range(S):
        for c in range(2):
            for at_row in (0, HALO + M):
                gmid[s, c, pl.ds(at_row, HALO), :] = zero
                for d in range(2):
                    grecv[d, s, c, pl.ds(at_row, HALO), :] = zero
    gp[...] = jnp.zeros(gp.shape, jnp.float32)

    pl.semaphore_wait(barrier, expected)

    def cor_copy(d):
        return pltpu.make_async_remote_copy(corv, cor_recv.at[d], corsem.at[0, d], corsem.at[1, d], **col_peer[d])

    def halo_copy(d):
        src, dst = ((0, HALO + TR), (TR - HALO, 0))[d]
        return pltpu.make_async_remote_copy(
            obj_hbm.at[:, pl.ds(src, HALO), :], ext.at[:, pl.ds(dst, HALO), :], yh.at[0, d], yh.at[1, d], **row_peer[d])

    for d in range(2):
        @pl.when(col_send[d])
        def _():
            cor_copy(d).start()

        @pl.when(row_send[d])
        def _():
            halo_copy(d).start()
    for d in range(2):
        @pl.when(col_recv[d])
        def _():
            cor_copy(d).wait_recv()
            c = pltpu.make_async_copy(cor_recv.at[d], cor_smem.at[d], cors.at[d])
            c.start()
            c.wait()
    locals_[0].wait()
    for d in range(2):
        @pl.when(row_recv[d])
        def _():
            halo_copy(d).wait_recv()

    def patch_copy(d, s):
        return pltpu.make_async_remote_copy(
            stage.at[d, s], nb.at[d, s], patsem.at[0, d, s], patsem.at[1, d, s], **col_peer[d])

    def grad_copy(d, s, c):
        return pltpu.make_async_remote_copy(
            gsend.at[d, s, c], grecv.at[d, s, c, pl.ds(HALO, M), :],
            gsem.at[0, d, s, c], gsem.at[1, d, s, c], **col_peer[d])

    for s in range(S):
        for d in range(2):
            @pl.when(col_send[d])
            def _():
                r = jnp.clip(cor_smem[1 - d, s, 0], 0, TR + 2 * HALO - M)
                for c in range(2):
                    stage[d, s, c] = ext[c, pl.ds(r, M), :]
                patch_copy(d, s).start()

    for c in locals_[1:]:
        c.wait()
    own_count = counts[grp * PN + pos]

    def slot(s, carry):
        r = jnp.clip(corners[0, s] - grp * TR + HALO, 0, TR + 2 * HALO - M)
        shift = jnp.clip(corners[1, s] - pos * HALO + HALO, 0, HALO)
        for d in range(2):
            @pl.when(col_recv[d])
            def _():
                patch_copy(d, s).wait_recv()
        back = lax.rem(HALO - shift, HALO)
        forth = lax.rem(shift, HALO)
        first = lane < HALO - shift
        patch = []
        for c in range(2):
            mid = pltpu.roll(ext[c, pl.ds(r, M), :], back, 1)
            before = pltpu.roll(nb[1, s, c], back, 1)
            after = pltpu.roll(nb[0, s, c], back, 1)
            patch.append(jnp.concatenate([jnp.where(first, before, mid), jnp.where(first, mid, after)], axis=1))
        pr, pi = prb[0], prb[1]
        wave = jnp.concatenate([pr * patch[0] - pi * patch[1], pr * patch[1] + pi * patch[0]], axis=0)
        front = table_left(tab, 0, wave)
        far = table_right(jnp.concatenate([front[:M], front[M:]], axis=1), tab, 1)
        fr, fi = far[:, :M], far[:, M:]
        excess = fr * fr + fi * fi - pat[s]
        excess = jnp.where(jnp.full((M, M), s, jnp.int32) < own_count, excess, 0.0)
        back_ = table_left(tab, 1, jnp.concatenate([excess * fr, excess * fi], axis=0))
        chi = table_right(jnp.concatenate([back_[:M], back_[M:]], axis=1), tab, 0)
        cr, ci = chi[:, :M], chi[:, M:]
        parts = (pr * cr + pi * ci, pr * ci - pi * cr)
        gp[0] += patch[0] * cr + patch[1] * ci
        gp[1] += patch[0] * ci - patch[1] * cr
        tail = lane >= shift
        for c in range(2):
            g0 = pltpu.roll(parts[c][:, :HALO], forth, 1)
            g1 = pltpu.roll(parts[c][:, HALO:], forth, 1)
            gsend[0, s, c] = jnp.where(tail, g0, 0.0)
            gmid[s, c, pl.ds(HALO, M), :] = jnp.where(tail, g1, g0)
            gsend[1, s, c] = jnp.where(tail, 0.0, g1)
        for d in range(2):
            @pl.when(col_send[d] & (s < S - 1))
            def _():
                grad_copy(d, s, 0).start()

            @pl.when(col_send[d] & (s < S - 2))
            def _():
                grad_copy(d, s, 1).start()
        return carry

    lax.fori_loop(0, S, slot, 0)

    core_copy = pltpu.make_async_remote_copy(
        gp.at[:, pl.ds((1 - core) * half, half), :], p1r, csem.at[0], csem.at[1], **partner)
    core_copy.start()
    core_copy.wait_recv()
    p1[...] = gp[:, pl.ds(pl.multiple_of(core * half, half), half), :] + p1r[...]

    def grp_copy(k):
        rows = pl.ds(pl.multiple_of(grp_at(k) * h2, h2), h2)
        return pltpu.make_async_remote_copy(
            p1.at[:, rows, :], p2r.at[k], gysem.at[0, k], gysem.at[1, k], **at(grp_at(k), pos))

    for k in range(1, G):
        grp_copy(k).start()

    for k in range(1, G):
        grp_copy(k).wait_recv()
    total = p1[:, pl.ds(pl.multiple_of(grp * h2, h2), h2), :]
    for k in range(1, G):
        total = total + p2r[k]
    p2[...] = total

    def share_copy(k):
        q = lax.rem(chip_at(k), owners)
        rows = pl.ds(pl.multiple_of(q * h3, 8), h3)
        return pltpu.make_async_remote_copy(
            p2.at[:, rows, :], p3r.at[k], asem.at[0, k], asem.at[1, k], **at(grp, chip_at(k) * 2 + core))

    for k in range(1, chips):
        @pl.when(chip_at(k) < owners)
        def _():
            share_copy(k).start()

    for d in range(2):
        @pl.when(col_send[d])
        def _():
            if S > 1:
                grad_copy(d, S - 2, 1).start()

    live = counts[0]
    for i in range(1, G * PN):
        live = live + counts[i]

    def new_rows(owner):
        return pl.ds(pl.multiple_of(core * half + grp * h2 + lax.rem(owner, owners) * h3, 8), h3)

    @pl.when(chip < owners)
    def _():
        total = p2[:, pl.ds(pl.multiple_of(lax.rem(chip, owners) * h3, 8), h3), :]
        for k in range(1, chips):
            share_copy(k).wait_recv()
            total = total + p3r[k]
        divisor = jnp.full(total.shape, live, jnp.int32).astype(jnp.float32)
        pnew[:, new_rows(chip), :] = prb[:, new_rows(chip), :] - STEP_PROBE * total / divisor

    def spread_copy(k, owner):
        return pltpu.make_async_remote_copy(
            pnew.at[:, new_rows(owner), :], pnew.at[:, new_rows(owner), :], agsem.at[0, k], agsem.at[1, k],
            **at(grp, chip_at(k) * 2 + core))

    @pl.when(chip < owners)
    def _():
        for k in range(1, chips):
            spread_copy(k, chip).start()
    for d in range(2):
        @pl.when(col_send[d])
        def _():
            for c in range(2):
                grad_copy(d, S - 1, c).start()

    for k in range(1, chips):
        source = lax.rem(chip + chips - k, chips)

        @pl.when(source < owners)
        def _():
            spread_copy(k, source).wait_recv()

    def grp_spread(k, g):
        rows = pl.ds(pl.multiple_of(core * half + g * h2, h2), h2)
        return pltpu.make_async_remote_copy(
            pnew.at[:, rows, :], pnew.at[:, rows, :], gasem.at[0, k], gasem.at[1, k], **at(grp_at(k), pos))

    for k in range(1, G):
        grp_spread(k, grp).start()

    for d in range(2):
        @pl.when(col_recv[d])
        def _():
            for s in range(S):
                for c in range(2):
                    grad_copy(d, s, c).wait_recv()

    def gather(base):
        totals = [jnp.zeros((HALO, HALO), jnp.float32)] * 2
        for s in range(S):
            off = jnp.clip(base - (corners[0, s] - grp * TR + HALO) + HALO, 0, HALO + M)
            totals = [totals[c] + gmid[s, c, pl.ds(off, HALO), :] for c in range(2)]
        for c in range(2):
            gacc[c, pl.ds(base, HALO), :] = totals[c]
        for d in range(2):
            @pl.when(col_recv[d])
            def _():
                for c in range(2):
                    total = gacc[c, pl.ds(base, HALO), :]
                    for s in range(S):
                        off = jnp.clip(base - cor_smem[d, s, 0] + HALO, 0, HALO + M)
                        total = total + grecv[d, s, c, pl.ds(off, HALO), :]
                    gacc[c, pl.ds(base, HALO), :] = total

    def gather_rim(chunk, carry):
        gather(pl.multiple_of(chunk * (TR + HALO), HALO))
        return carry

    def gather_core(chunk, carry):
        base = pl.multiple_of(chunk * HALO + HALO, HALO)
        gather(base)
        for c in range(2):
            obj_out[c, pl.ds(pl.multiple_of(chunk * HALO, HALO), HALO), :] = (
                ext[c, pl.ds(base, HALO), :] - STEP_OBJECT * gacc[c, pl.ds(base, HALO), :])
        return carry

    lax.fori_loop(0, 2, gather_rim, 0)

    def rim_copy(d):
        src = (0, HALO + TR)[d]
        return pltpu.make_async_remote_copy(
            gacc.at[:, pl.ds(src, HALO), :], yrecv.at[d], ysem.at[0, d], ysem.at[1, d], **row_peer[d])

    for d in range(2):
        @pl.when(row_send[d])
        def _():
            rim_copy(d).start()

    for k in range(1, G):
        grp_spread(k, lax.rem(grp + G - k, G)).wait_recv()

    def core_spread(c):
        rows = pl.ds(pl.multiple_of(c * half, half), half)
        return pltpu.make_async_remote_copy(pnew.at[:, rows, :], pnew.at[:, rows, :], casem.at[0], casem.at[1], **partner)

    core_spread(core).start()

    lax.fori_loop(0, TR // HALO, gather_core, 0)
    for d in range(2):
        @pl.when(row_recv[d])
        def _():
            rim_copy(d).wait_recv()
            rows = pl.ds((TR - HALO, 0)[d], HALO)
            obj_out[:, rows, :] = obj_out[:, rows, :] - STEP_OBJECT * yrecv[d]

    core_spread(1 - core).wait_recv()
    prb_out[...] = pnew[...]

    for d in range(2):
        @pl.when(col_send[d])
        def _():
            cor_copy(d).wait_send()
            for s in range(S):
                patch_copy(d, s).wait_send()
                for c in range(2):
                    grad_copy(d, s, c).wait_send()

        @pl.when(row_send[d])
        def _():
            halo_copy(d).wait_send()
            rim_copy(d).wait_send()
    core_copy.wait_send()
    for k in range(1, G):
        grp_copy(k).wait_send()
        grp_spread(k, grp).wait_send()
    for k in range(1, chips):
        @pl.when(chip_at(k) < owners)
        def _():
            share_copy(k).wait_send()

        @pl.when(chip < owners)
        def _():
            spread_copy(k, chip).wait_send()
    core_spread(core).wait_send()


def on_device(grp_size, pos_size, tables, object_field, probe_field, patterns, corners, counts):
    TR, S, M = object_field.shape[1], patterns.shape[0], probe_field.shape[1]
    chips, half = pos_size // 2, M // 2
    h2 = half // grp_size
    h3 = max(8, h2 // chips)
    f32 = jnp.float32
    V, D = pltpu.VMEM, pltpu.SemaphoreType.DMA
    smem = pl.BlockSpec(memory_space=pltpu.SMEM)
    hbm = pl.BlockSpec(memory_space=pl.ANY)
    vmem = pl.BlockSpec(memory_space=pltpu.VMEM)
    return pl.pallas_call(
        functools.partial(kernel, (grp_size, pos_size, S, TR, M)),
        out_shape=(
            pltpu.VMEM(object_field.shape, f32),
            pltpu.VMEM(probe_field.shape, f32),
        ),
        in_specs=[smem, smem, hbm, hbm, hbm, hbm],
        out_specs=(vmem, vmem),
        scratch_shapes=[
            V((2, TR + 2 * HALO, HALO), f32),
            V((2, M, M), f32),
            V((S, M, M), f32),
            V(tables.shape, jnp.bfloat16),
            V((2, S, 2, M, HALO), f32),
            V((2, S, 2, M, HALO), f32),
            V((8, 128), jnp.int32),
            V((2, 8, 128), jnp.int32),
            pltpu.SMEM((2, 8, 128), jnp.int32),
            V((S, 2, M + 2 * HALO, HALO), f32),
            V((2, S, 2, M, HALO), f32),
            V((2, S, 2, M + 2 * HALO, HALO), f32),
            V((2, TR + 2 * HALO, HALO), f32),
            V((2, 2, HALO, HALO), f32),
            V((2, M, M), f32),
            V((2, half, M), f32),
            V((2, half, M), f32),
            V((grp_size, 2, h2, M), f32),
            V((2, h2, M), f32),
            V((chips, 2, h3, M), f32),
            V((2, M, M), f32),
            D((4,)), D((2, 2)), D((2, 2)), D((2,)), D((2, 2, S)), D((2, 2, S, 2)), D((2, 2)), D((2,)),
            D((2, grp_size)), D((2, chips)), D((2, chips)), D((2, grp_size)), D((2,)),
        ],
        compiler_params=pltpu.CompilerParams(
            collective_id=0, has_side_effects=True, vmem_limit_bytes=56 * 1024 * 1024
        ),
    )(corners, counts, object_field, probe_field, patterns, jnp.asarray(tables))


def solution(mesh):
    def body(object_field, probe_field, patterns, corners, counts):
        tables = dft_tables(probe_field.shape[1])
        return on_device(
            mesh.shape["grp"], mesh.shape["pos"], tables, object_field, probe_field, patterns, corners, counts
        )

    return jax.shard_map(
        body,
        mesh=mesh,
        in_specs=(
            P(None, "grp", "pos"),
            P(),
            P(("grp", "pos"), None, None),
            P(None, ("grp", "pos")),
            P(),
        ),
        out_specs=(P(None, "grp", "pos"), P()),
        check_vma=False,
    )
```

profile of v0, /device:TPU:0, one launch (start us, length us, event | category | flops | bytes accessed | tf_op | source)
XLA Modules:
  0.0 63.4 jit_solution(11754039156457071260)
XLA Ops:
  0.6 61.0 %shard_map.77 = (f32[2,1024,128]{2,1,0:T(8,128)S(1)}, f32[2,256,256]{2,1,0:T(8,128)S(1)}) custom-call(s32[2,3]{1,0:T(2,128)} %corners.1, s32[32]{0:T(128)} %counts.1, f32[2,1024,128]{2,1,0:T(8,128)} %obj_hbm.1, f32[2,256,256]{2,1,0:T(8,128)} %prb_hbm.1, f32[3,256,256]{2,1,0:T(8,128)} %pat_hbm.1, bf16[2,2,512,512]{3,2,1,0:T(8,128)(2,1)} %constant.2.clone.tab_hbm), custom_call_target="tpu_custom_call" | custom-call | tf_op jit(solution)/shard_map/pallas_call | solution.py:406
  61.7 1.0 %copy.10 = f32[2,1024,128]{2,1,0:T(8,128)} copy(f32[2,1024,128]{2,1,0:T(8,128)S(1)} %get-tuple-element.2) | data formatting | bytes 2097152
  62.6 0.8 %copy.11 = f32[2,256,256]{2,1,0:T(8,128)} copy(f32[2,256,256]{2,1,0:T(8,128)S(1)} %get-tuple-element.3) | data formatting | bytes 1048576
where the time goes:
time: 63.6 us; the launch traced here: 63.4 us
  Pallas kernels  61 us (96%)
  local copies, waits for them, and re-layouts  1.77 us (3%)
  between operations  0.64 us (1%)
    pallas_call x1, Pallas kernels, on_device(): pl.pallas_call(functools.partial(kernel, (grp_size, pos_size, S, TR, M)),...  61 us
    unnamed x2, local copies, waits for them, and re-layouts  1.77 us

commit v1 on v0

--- a/solution.py
+++ b/solution.py
@@ -49,17 +49,24 @@
     return dot(high, th) + (dot(low, th) + dot(high, tl))
 
 
+def shares(rows, ring):
+    owners = min(ring, rows // 8)
+    return owners, rows // owners
+
+
 def kernel(sizes, corners, counts, obj_hbm, prb_hbm, pat_hbm, tab_hbm, obj_out, prb_out,
            ext, prb, pat, tab, nb, stage, corv, cor_recv, cor_smem,
-           gmid, gsend, grecv, gacc, yrecv, gp, p1r, p1, p2r, p2, p3r, pnew,
-           loc, yh, corsem, cors, patsem, gsem, ysem, csem, gysem, asem, agsem, gasem, casem):
+           gmid, gsend, grecv, gacc, yrecv, gp, p1r, p1, p3r, p2, p2x, pnew,
+           loc, yh, corsem, cors, patsem, gsem, ysem, csem, asem, agsem, xsem, casem):
     G, PN, S, TR, M = sizes
     grp, pos = lax.axis_index("grp"), lax.axis_index("pos")
     core, chip, chips = lax.rem(pos, 2), pos // 2, PN // 2
     half = M // 2
-    h2 = half // G
-    h3 = max(8, h2 // chips)
-    owners = h2 // h3
+    side, lines = lax.rem(chip, 2), chips // 2
+    ring = G * lines
+    owners, h3 = shares(half, ring)
+    me = grp * lines + chip // 2
+    late = side != core
 
     def at(g, p):
         return {"device_id": (g, p), "device_id_type": MESH}
@@ -70,11 +77,14 @@
     row_send, row_recv = [grp > 0, grp < G - 1], [grp < G - 1, grp > 0]
     partner = at(grp, pos + 1 - 2 * core)
 
-    def grp_at(k):
-        return lax.rem(grp + k, G)
-
-    def chip_at(k):
-        return lax.rem(chip + k, chips)
+    across = at(grp, pos + 2 - 4 * side)
+
+    def ring_at(k):
+        return lax.rem(me + k, ring)
+
+    def ring_peer(k):
+        q = ring_at(k)
+        return at(q // lines, (lax.rem(q, lines) * 2 + side) * 2 + core)
 
     locals_ = [
         pltpu.make_async_copy(obj_hbm, ext.at[:, pl.ds(HALO, TR), :], loc.at[0]),
@@ -90,12 +100,10 @@
         @pl.when(col_send[d])
         def _():
             pl.semaphore_signal(barrier, inc=1, **col_peer[d])
-    for k in range(1, G):
-        pl.semaphore_signal(barrier, inc=1, **at(grp_at(k), pos))
-    for k in range(1, chips):
-        pl.semaphore_signal(barrier, inc=1, **at(grp, chip_at(k) * 2 + core))
-    pl.semaphore_signal(barrier, inc=1, **partner)
-    expected = (pos > 0).astype(jnp.int32) + (pos < PN - 1).astype(jnp.int32) + G + chips - 1
+    for k in range(1, ring):
+        pl.semaphore_signal(barrier, inc=1, **ring_peer(k))
+    pl.semaphore_signal(barrier, inc=1, **across)
+    expected = (pos > 0).astype(jnp.int32) + (pos < PN - 1).astype(jnp.int32) + ring
 
     lane = lax.broadcasted_iota(jnp.int32, (M, HALO), 1)
     row8 = lax.broadcasted_iota(jnp.int32, (8, 128), 0)
@@ -117,6 +125,9 @@
     def cor_copy(d):
         return pltpu.make_async_remote_copy(corv, cor_recv.at[d], corsem.at[0, d], corsem.at[1, d], **col_peer[d])
 
+    def cor_local(d):
+        return pltpu.make_async_copy(cor_recv.at[d], cor_smem.at[d], cors.at[d])
+
     def halo_copy(d):
         src, dst = ((0, HALO + TR), (TR - HALO, 0))[d]
         return pltpu.make_async_remote_copy(
@@ -134,9 +145,11 @@
         @pl.when(col_recv[d])
         def _():
             cor_copy(d).wait_recv()
-            c = pltpu.make_async_copy(cor_recv.at[d], cor_smem.at[d], cors.at[d])
-            c.start()
-            c.wait()
+            cor_local(d).start()
+    for d in range(2):
+        @pl.when(col_recv[d])
+        def _():
+            cor_local(d).wait()
     locals_[0].wait()
     for d in range(2):
         @pl.when(row_recv[d])
@@ -202,13 +215,10 @@
             gmid[s, c, pl.ds(HALO, M), :] = jnp.where(tail, g1, g0)
             gsend[1, s, c] = jnp.where(tail, 0.0, g1)
         for d in range(2):
-            @pl.when(col_send[d] & (s < S - 1))
+            @pl.when(col_send[d] & ((core != d) | (late & (s < S - 1))))
             def _():
-                grad_copy(d, s, 0).start()
-
-            @pl.when(col_send[d] & (s < S - 2))
-            def _():
-                grad_copy(d, s, 1).start()
+                for c in range(2):
+                    grad_copy(d, s, c).start()
         return carry
 
     lax.fori_loop(0, S, slot, 0)
@@ -216,93 +226,93 @@
     core_copy = pltpu.make_async_remote_copy(
         gp.at[:, pl.ds((1 - core) * half, half), :], p1r, csem.at[0], csem.at[1], **partner)
     core_copy.start()
-    core_copy.wait_recv()
-    p1[...] = gp[:, pl.ds(pl.multiple_of(core * half, half), half), :] + p1r[...]
-
-    def grp_copy(k):
-        rows = pl.ds(pl.multiple_of(grp_at(k) * h2, h2), h2)
-        return pltpu.make_async_remote_copy(
-            p1.at[:, rows, :], p2r.at[k], gysem.at[0, k], gysem.at[1, k], **at(grp_at(k), pos))
-
-    for k in range(1, G):
-        grp_copy(k).start()
-
-    for k in range(1, G):
-        grp_copy(k).wait_recv()
-    total = p1[:, pl.ds(pl.multiple_of(grp * h2, h2), h2), :]
-    for k in range(1, G):
-        total = total + p2r[k]
-    p2[...] = total
-
-    def share_copy(k):
-        q = lax.rem(chip_at(k), owners)
-        rows = pl.ds(pl.multiple_of(q * h3, 8), h3)
-        return pltpu.make_async_remote_copy(
-            p2.at[:, rows, :], p3r.at[k], asem.at[0, k], asem.at[1, k], **at(grp, chip_at(k) * 2 + core))
-
-    for k in range(1, chips):
-        @pl.when(chip_at(k) < owners)
-        def _():
-            share_copy(k).start()
-
-    for d in range(2):
-        @pl.when(col_send[d])
-        def _():
-            if S > 1:
-                grad_copy(d, S - 2, 1).start()
+
+    def held(first, which):
+        for d in range(2):
+            @pl.when(col_send[d] & (core == d) & which)
+            def _():
+                for s in range(first, S):
+                    for c in range(2):
+                        grad_copy(d, s, c).start()
+
+    for d in range(2):
+        @pl.when(col_recv[d] & (core == d))
+        def _():
+            for s in range(S - 1):
+                for c in range(2):
+                    grad_copy(d, s, c).wait_recv()
+    held(0, ~late)
 
     live = counts[0]
     for i in range(1, G * PN):
         live = live + counts[i]
 
+    core_copy.wait_recv()
+    p1[...] = gp[:, pl.ds(pl.multiple_of(core * half, half), half), :] + p1r[...]
+
+    def share_rows(q):
+        return pl.ds(pl.multiple_of(lax.rem(q, owners) * h3, 8), h3)
+
+    def share_copy(k):
+        return pltpu.make_async_remote_copy(
+            p1.at[:, share_rows(ring_at(k)), :], p3r.at[k], asem.at[0, k], asem.at[1, k], **ring_peer(k))
+
+    for k in range(1, ring):
+        @pl.when(ring_at(k) < owners)
+        def _():
+            share_copy(k).start()
+
     def new_rows(owner):
-        return pl.ds(pl.multiple_of(core * half + grp * h2 + lax.rem(owner, owners) * h3, 8), h3)
-
-    @pl.when(chip < owners)
+        return pl.ds(pl.multiple_of(core * half + lax.rem(owner, owners) * h3, 8), h3)
+
+    across_copy = pltpu.make_async_remote_copy(p2, p2x, xsem.at[0], xsem.at[1], **across)
+
+    @pl.when(me < owners)
     def _():
-        total = p2[:, pl.ds(pl.multiple_of(lax.rem(chip, owners) * h3, 8), h3), :]
-        for k in range(1, chips):
+        total = p1[:, share_rows(me), :]
+        for k in range(1, ring):
             share_copy(k).wait_recv()
             total = total + p3r[k]
+        p2[...] = total
+        across_copy.start()
+
+    held(S - 1, late)
+
+    def spread_copy(k, owner):
+        return pltpu.make_async_remote_copy(
+            pnew.at[:, new_rows(owner), :], pnew.at[:, new_rows(owner), :], agsem.at[0, k], agsem.at[1, k],
+            **ring_peer(k))
+
+    @pl.when(me < owners)
+    def _():
+        across_copy.wait_recv()
+        total = p2[...] + p2x[...]
         divisor = jnp.full(total.shape, live, jnp.int32).astype(jnp.float32)
-        pnew[:, new_rows(chip), :] = prb[:, new_rows(chip), :] - STEP_PROBE * total / divisor
-
-    def spread_copy(k, owner):
-        return pltpu.make_async_remote_copy(
-            pnew.at[:, new_rows(owner), :], pnew.at[:, new_rows(owner), :], agsem.at[0, k], agsem.at[1, k],
-            **at(grp, chip_at(k) * 2 + core))
-
-    @pl.when(chip < owners)
-    def _():
-        for k in range(1, chips):
-            spread_copy(k, chip).start()
-    for d in range(2):
-        @pl.when(col_send[d])
-        def _():
-            for c in range(2):
-                grad_copy(d, S - 1, c).start()
-
-    for k in range(1, chips):
-        source = lax.rem(chip + chips - k, chips)
+        pnew[:, new_rows(me), :] = prb[:, new_rows(me), :] - STEP_PROBE * total / divisor
+        for k in range(1, ring):
+            spread_copy(k, me).start()
+
+    for k in range(1, ring):
+        source = lax.rem(me + ring - k, ring)
 
         @pl.when(source < owners)
         def _():
             spread_copy(k, source).wait_recv()
 
-    def grp_spread(k, g):
-        rows = pl.ds(pl.multiple_of(core * half + g * h2, h2), h2)
-        return pltpu.make_async_remote_copy(
-            pnew.at[:, rows, :], pnew.at[:, rows, :], gasem.at[0, k], gasem.at[1, k], **at(grp_at(k), pos))
-
-    for k in range(1, G):
-        grp_spread(k, grp).start()
+    def core_spread(c):
+        rows = pl.ds(pl.multiple_of(c * half, half), half)
+        return pltpu.make_async_remote_copy(pnew.at[:, rows, :], pnew.at[:, rows, :], casem.at[0], casem.at[1], **partner)
+
+    core_spread(core).start()
 
     for d in range(2):
         @pl.when(col_recv[d])
         def _():
             for s in range(S):
-                for c in range(2):
-                    grad_copy(d, s, c).wait_recv()
+                @pl.when((core != d) | (s == S - 1))
+                def _():
+                    for c in range(2):
+                        grad_copy(d, s, c).wait_recv()
 
     def gather(base):
         totals = [jnp.zeros((HALO, HALO), jnp.float32)] * 2
@@ -345,15 +355,6 @@
         def _():
             rim_copy(d).start()
 
-    for k in range(1, G):
-        grp_spread(k, lax.rem(grp + G - k, G)).wait_recv()
-
-    def core_spread(c):
-        rows = pl.ds(pl.multiple_of(c * half, half), half)
-        return pltpu.make_async_remote_copy(pnew.at[:, rows, :], pnew.at[:, rows, :], casem.at[0], casem.at[1], **partner)
-
-    core_spread(core).start()
-
     lax.fori_loop(0, TR // HALO, gather_core, 0)
     for d in range(2):
         @pl.when(row_recv[d])
@@ -379,25 +380,26 @@
             halo_copy(d).wait_send()
             rim_copy(d).wait_send()
     core_copy.wait_send()
-    for k in range(1, G):
-        grp_copy(k).wait_send()
-        grp_spread(k, grp).wait_send()
-    for k in range(1, chips):
-        @pl.when(chip_at(k) < owners)
+
+    @pl.when(me < owners)
+    def _():
+        across_copy.wait_send()
+    for k in range(1, ring):
+        @pl.when(ring_at(k) < owners)
         def _():
             share_copy(k).wait_send()
 
-        @pl.when(chip < owners)
-        def _():
-            spread_copy(k, chip).wait_send()
+        @pl.when(me < owners)
+        def _():
+            spread_copy(k, me).wait_send()
     core_spread(core).wait_send()
 
 
 def on_device(grp_size, pos_size, tables, object_field, probe_field, patterns, corners, counts):
     TR, S, M = object_field.shape[1], patterns.shape[0], probe_field.shape[1]
     chips, half = pos_size // 2, M // 2
-    h2 = half // grp_size
-    h3 = max(8, h2 // chips)
+    ring = grp_size * (chips // 2)
+    owners, h3 = shares(half, ring)
     f32 = jnp.float32
     V, D = pltpu.VMEM, pltpu.SemaphoreType.DMA
     smem = pl.BlockSpec(memory_space=pltpu.SMEM)
@@ -429,12 +431,12 @@
             V((2, M, M), f32),
             V((2, half, M), f32),
             V((2, half, M), f32),
-            V((grp_size, 2, h2, M), f32),
-            V((2, h2, M), f32),
-            V((chips, 2, h3, M), f32),
+            V((ring, 2, h3, M), f32),
+            V((2, h3, M), f32),
+            V((2, h3, M), f32),
             V((2, M, M), f32),
             D((4,)), D((2, 2)), D((2, 2)), D((2,)), D((2, 2, S)), D((2, 2, S, 2)), D((2, 2)), D((2,)),
-            D((2, grp_size)), D((2, chips)), D((2, chips)), D((2, grp_size)), D((2,)),
+            D((2, ring)), D((2, ring)), D((2,)), D((2,)),
         ],
         compiler_params=pltpu.CompilerParams(
             collective_id=0, has_side_effects=True, vmem_limit_bytes=56 * 1024 * 1024

time: 63.6 us -> 62.2 us (0.978)
  Pallas kernels: 61 us -> 59.1 us
    pallas_call x1, Pallas kernels: 61 us -> 59.1 us  [on_device(): pl.pallas_call(functools.partial(kernel, (grp_size, pos_size, S, TR, M)),...]
where the time goes in v1:
time: 62.2 us; the launch traced here: 61.5 us
  Pallas kernels  59.1 us (95%)
  local copies, waits for them, and re-layouts  1.77 us (3%)
  between operations  0.64 us (1%)
    pallas_call x1, Pallas kernels, on_device(): pl.pallas_call(functools.partial(kernel, (grp_size, pos_size, S, TR, M)),...  59.1 us
    unnamed x2, local copies, waits for them, and re-layouts  1.77 us

profile of v1, /device:TPU:0, one launch (start us, length us, event | category | flops | bytes accessed | tf_op | source)
XLA Modules:
  0.0 61.5 jit_solution(16349568530456930915)
XLA Ops:
  0.6 59.1 %shard_map.77 = (f32[2,1024,128]{2,1,0:T(8,128)S(1)}, f32[2,256,256]{2,1,0:T(8,128)S(1)}) custom-call(s32[2,3]{1,0:T(2,128)} %corners.1, s32[32]{0:T(128)} %counts.1, f32[2,1024,128]{2,1,0:T(8,128)} %obj_hbm.1, f32[2,256,256]{2,1,0:T(8,128)} %prb_hbm.1, f32[3,256,256]{2,1,0:T(8,128)} %pat_hbm.1, bf16[2,2,512,512]{3,2,1,0:T(8,128)(2,1)} %constant.2.clone.tab_hbm), custom_call_target="tpu_custom_call" | custom-call | tf_op jit(solution)/shard_map/pallas_call | solution.py:408
  59.8 1.0 %copy.10 = f32[2,1024,128]{2,1,0:T(8,128)} copy(f32[2,1024,128]{2,1,0:T(8,128)S(1)} %get-tuple-element.2) | data formatting | bytes 2097152
  60.7 0.8 %copy.11 = f32[2,256,256]{2,1,0:T(8,128)} copy(f32[2,256,256]{2,1,0:T(8,128)S(1)} %get-tuple-element.3) | data formatting | bytes 1048576

commit v2 on v1

v2 whole, which is shorter than its diff:
```python
import functools

import jax
import jax.numpy as jnp
import numpy as np
from jax import lax
from jax.experimental import pallas as pl
from jax.experimental.pallas import tpu as pltpu
from jax.sharding import PartitionSpec as P

HALO = 128
STEP_OBJECT = 0.25
STEP_PROBE = 4.0
MESH = pl.DeviceIdType.MESH


def dft_tables(order):
    half = order // 2
    columns = np.arange(half, dtype=np.int64)
    tables = []
    for odd in range(2):
        rows = 2 * np.arange(half, dtype=np.int64) + odd
        angles = (rows[:, None] * columns[None, :] % order) * (2.0 * np.pi / order)
        re, im = np.cos(angles) / np.sqrt(order), -np.sin(angles) / np.sqrt(order)
        block = np.block([[re, -im], [im, re]])
        tables.append(np.stack([block, block.T]))
    both = np.stack(tables).astype(np.float32)
    high = both.astype(jnp.bfloat16)
    low = (both - high.astype(np.float32)).astype(jnp.bfloat16)
    return np.stack([high, low], axis=2)


def split(x):
    high = x.astype(jnp.bfloat16)
    low = (x - high.astype(jnp.float32)).astype(jnp.bfloat16)
    return high, low


def dot(a, b):
    return jnp.dot(a, b, preferred_element_type=jnp.float32)


def table_left(tab, odd, turn, data):
    high, low = split(data)
    th, tl = tab[odd, turn, 0], tab[odd, turn, 1]
    return dot(th, high) + (dot(th, low) + dot(tl, high))


def table_right(data, tab, odd, turn):
    high, low = split(data)
    th, tl = tab[odd, turn, 0], tab[odd, turn, 1]
    return dot(high, th) + (dot(low, th) + dot(high, tl))


def rows_of(x, h):
    n = x.shape[0] // 2
    return x[h * n : (h + 1) * n]


def cols_of(x, h):
    n = x.shape[1] // 2
    return x[:, h * n : (h + 1) * n]


def stack(a, b):
    return jnp.concatenate([a, b], axis=0)


def side_by_side(a, b):
    return jnp.concatenate([a, b], axis=1)


def forward(tab, re, im):
    r0, r1, i0, i1 = rows_of(re, 0), rows_of(re, 1), rows_of(im, 0), rows_of(im, 1)
    even = table_left(tab, 0, 0, stack(r0 + r1, i0 + i1))
    odd = table_left(tab, 1, 0, stack(r0 - r1, i0 - i1))
    re, im = stack(rows_of(even, 0), rows_of(odd, 0)), stack(rows_of(even, 1), rows_of(odd, 1))
    r0, r1, i0, i1 = cols_of(re, 0), cols_of(re, 1), cols_of(im, 0), cols_of(im, 1)
    even = table_right(side_by_side(r0 + r1, i0 + i1), tab, 0, 1)
    odd = table_right(side_by_side(r0 - r1, i0 - i1), tab, 1, 1)
    return side_by_side(cols_of(even, 0), cols_of(odd, 0)), side_by_side(cols_of(even, 1), cols_of(odd, 1))


def backward(tab, re, im):
    even = table_left(tab, 0, 1, stack(rows_of(re, 0), rows_of(im, 0)))
    odd = table_left(tab, 1, 1, stack(rows_of(re, 1), rows_of(im, 1)))
    total, rest = even + odd, even - odd
    re, im = stack(rows_of(total, 0), rows_of(rest, 0)), stack(rows_of(total, 1), rows_of(rest, 1))
    even = table_right(side_by_side(cols_of(re, 0), cols_of(im, 0)), tab, 0, 0)
    odd = table_right(side_by_side(cols_of(re, 1), cols_of(im, 1)), tab, 1, 0)
    total, rest = even + odd, even - odd
    return side_by_side(cols_of(total, 0), cols_of(rest, 0)), side_by_side(cols_of(total, 1), cols_of(rest, 1))


def shares(rows, ring):
    owners = min(ring, rows // 8)
    return owners, rows // owners


def kernel(sizes, corners, counts, obj_hbm, prb_hbm, pat_hbm, tab_hbm, obj_out, prb_out,
           ext, prb, pat, patp, tab, nb, stage, corv, cor_recv, cor_smem,
           gmid, gsend, grecv, relay, turned, rim, yrecv, gp, p1r, p3r, p2, p2x, pnew,
           loc, yh, corsem, cors, patsem, gsem, rsem, fsem, ysem, csem, asem, agsem, xsem, casem):
    G, PN, S, TR, M = sizes
    grp, pos = lax.axis_index("grp"), lax.axis_index("pos")
    core, chip, chips = lax.rem(pos, 2), pos // 2, PN // 2
    side, lines = lax.rem(chip, 2), chips // 2
    ring = G * lines
    owners, h3 = shares(M, ring)
    me = grp * lines + chip // 2
    late = side != core
    blocks = TR // HALO + 2

    def at(g, p):
        return {"device_id": (g, lax.rem(p + PN, PN)), "device_id_type": MESH}

    col_peer = [at(grp, pos - 1), at(grp, pos + 1)]
    row_peer = [at(lax.rem(grp + G - 1, G), pos), at(lax.rem(grp + 1, G), pos)]
    col_send, col_recv = [pos > 0, pos < PN - 1], [pos < PN - 1, pos > 0]
    row_send, row_recv = [grp > 0, grp < G - 1], [grp < G - 1, grp > 0]
    partner = at(grp, pos + 1 - 2 * core)
    across = at(grp, pos + 2 * core - 1)
    has_outer = ((core == 0) & (pos > 0)) | ((core == 1) & (pos < PN - 1))
    has_relay = late & (((core == 1) & (pos + 3 < PN)) | ((core == 0) & (pos >= 3)))
    relay_peer, feeder = at(grp, pos + 6 * core - 3), at(grp, pos + 2 - 4 * core)
    forward_peer = at(grp, pos + 4 * core - 2)

    def ring_at(k):
        return lax.rem(me + k, ring)

    def ring_peer(k):
        q = ring_at(k)
        return at(q // lines, (lax.rem(q, lines) * 2 + side) * 2 + core)

    locals_ = [
        pltpu.make_async_copy(obj_hbm, ext.at[:, pl.ds(HALO, TR), :], loc.at[0]),
        pltpu.make_async_copy(prb_hbm, prb, loc.at[1]),
        pltpu.make_async_copy(tab_hbm, tab, loc.at[2]),
    ] + [
        pltpu.make_async_copy(pat_hbm.at[:, :, pl.ds(w * HALO, HALO)], pat.at[w], loc.at[3 + w])
        for w in range(2)
    ]
    for c in locals_:
        c.start()

    barrier = pltpu.get_barrier_semaphore()

    def greet(condition, peers):
        @pl.when(condition)
        def _():
            for peer in peers:
                pl.semaphore_signal(barrier, inc=1, **peer)
        return condition.astype(jnp.int32) * len(peers)

    expected = greet(col_send[0], [col_peer[0]]) + greet(col_send[1], [col_peer[1]])
    expected += greet(~late & row_send[0], [row_peer[0]]) + greet(~late & row_send[1], [row_peer[1]])
    expected += greet(late, [ring_peer(k) for k in range(1, ring)])
    expected += greet(~late & has_outer, [relay_peer, feeder]) + greet(has_relay, [relay_peer, forward_peer])

    lane = lax.broadcasted_iota(jnp.int32, (M, HALO), 1)
    row8 = lax.broadcasted_iota(jnp.int32, (8, 128), 0)
    packed = jnp.zeros((8, 128), jnp.int32)
    for s in range(S):
        packed = jnp.where(row8 == s, corners[0, s] - grp * TR + HALO, packed)
    corv[...] = packed
    gp[...] = jnp.zeros(gp.shape, jnp.float32)

    pl.semaphore_wait(barrier, expected)

    def cor_copy(d):
        return pltpu.make_async_remote_copy(corv, cor_recv.at[d], corsem.at[0, d], corsem.at[1, d], **col_peer[d])

    def cor_local(d):
        return pltpu.make_async_copy(cor_recv.at[d], cor_smem.at[d], cors.at[d])

    def halo_copy(d):
        src, dst = ((0, HALO + TR), (TR - HALO, 0))[d]
        return pltpu.make_async_remote_copy(
            obj_hbm.at[:, pl.ds(src, HALO), :], ext.at[:, pl.ds(dst, HALO), :], yh.at[0, d], yh.at[1, d], **row_peer[d])

    for d in range(2):
        @pl.when(col_send[d])
        def _():
            cor_copy(d).start()

        @pl.when(row_send[d])
        def _():
            halo_copy(d).start()
    for d in range(2):
        @pl.when(col_recv[d])
        def _():
            cor_copy(d).wait_recv()
            cor_local(d).start()
    for d in range(2):
        @pl.when(col_recv[d])
        def _():
            cor_local(d).wait()
    locals_[0].wait()
    for d in range(2):
        @pl.when(row_recv[d])
        def _():
            halo_copy(d).wait_recv()

    def patch_copy(d, s):
        return pltpu.make_async_remote_copy(
            stage.at[d, s], nb.at[d, s], patsem.at[0, d, s], patsem.at[1, d, s], **col_peer[d])

    for s in range(S):
        for d in range(2):
            @pl.when(col_send[d])
            def _():
                r = jnp.clip(cor_smem[1 - d, s, 0], 0, TR + 2 * HALO - M)
                for c in range(2):
                    stage[d, s, c] = ext[c, pl.ds(r, M), :]
                patch_copy(d, s).start()

    def grad_to(d, s, h, peer):
        return pltpu.make_async_remote_copy(
            gsend.at[d, s, h], grecv.at[d, s, h], gsem.at[0, d, s, h], gsem.at[1, d, s, h], **peer)

    def chip_grad(s, h):
        return grad_to(1 - core, s, h, partner)

    def outer_grad(s, h):
        return grad_to(core, s, h, across)

    def relay_grad(s, h):
        return pltpu.make_async_remote_copy(
            gsend.at[core, s, h], relay.at[s, h], gsem.at[0, core, s, h], rsem.at[s, h], **relay_peer)

    def forward_grad(s, h):
        return pltpu.make_async_remote_copy(
            relay.at[s, h], grecv.at[1 - core, s, h], fsem.at[s, h], gsem.at[1, 1 - core, s, h], **forward_peer)

    first_half = (grp < G - 1).astype(jnp.int32)
    halves = [first_half, 1 - first_half]

    for c in locals_[1:]:
        c.wait()
    own_count = counts[grp * PN + pos]

    column = lax.broadcasted_iota(jnp.int32, (M, M), 1)
    wanted = jnp.where(column < M // 2, 2 * column, 2 * column - (M - 1))
    pick = (lax.broadcasted_iota(jnp.int32, (M, M), 0) == wanted).astype(jnp.float32).astype(jnp.bfloat16)

    def reorder(s, carry):
        rows = side_by_side(*[
            stack(*[pat[w, s, pl.ds(odd, M // 2, stride=2), :] for odd in range(2)]) for w in range(2)
        ])
        high, low = split(rows)
        last = (rows - high.astype(jnp.float32) - low.astype(jnp.float32)).astype(jnp.bfloat16)
        patp[s] = dot(high, pick) + (dot(low, pick) + dot(last, pick))
        return carry

    lax.fori_loop(0, S, reorder, 0)

    def row_of(s):
        return jnp.clip(corners[0, s] - grp * TR + HALO, 0, TR + 2 * HALO - M)

    def slot(s, carry):
        r = row_of(s)
        shift = jnp.clip(corners[1, s] - pos * HALO + HALO, 0, HALO)
        for d in range(2):
            @pl.when(col_recv[d])
            def _():
                patch_copy(d, s).wait_recv()
        back = lax.rem(HALO - shift, HALO)
        forth = lax.rem(shift, HALO)
        first = lane < HALO - shift
        patch = []
        for c in range(2):
            mid = pltpu.roll(ext[c, pl.ds(r, M), :], back, 1)
            before = pltpu.roll(nb[1, s, c], back, 1)
            after = pltpu.roll(nb[0, s, c], back, 1)
            patch.append(side_by_side(jnp.where(first, before, mid), jnp.where(first, mid, after)))
        pr, pi = prb[0], prb[1]
        fr, fi = forward(tab, pr * patch[0] - pi * patch[1], pr * patch[1] + pi * patch[0])
        excess = fr * fr + fi * fi - patp[s]
        excess = jnp.where(jnp.full((M, M), s, jnp.int32) < own_count, excess, 0.0)
        cr, ci = backward(tab, excess * fr, excess * fi)
        parts = (pr * cr + pi * ci, pr * ci - pi * cr)
        gp[0] += patch[0] * cr + patch[1] * ci
        gp[1] += patch[0] * ci - patch[1] * cr
        tail = lane >= shift
        for c in range(2):
            for w in range(2):
                turned[c, w, :M] = cols_of(parts[c], w)
                turned[c, w, M:] = cols_of(parts[c], w)
        start = M - lax.rem(r, M)
        for c in range(2):
            g0, g1 = [pltpu.roll(turned[c, w, pl.ds(start, M), :], forth, 1) for w in range(2)]
            left, middle, right = jnp.where(tail, g0, 0.0), jnp.where(tail, g1, g0), jnp.where(tail, 0.0, g1)
            for h in range(2):
                gsend[0, s, h, c] = rows_of(left, h)
                gmid[s, h, c] = rows_of(middle, h)
                gsend[1, s, h, c] = rows_of(right, h)
        for h in range(2):
            chip_grad(s, h).start()

        @pl.when(has_outer & late)
        def _():
            outer_grad(s, halves[0]).start()

        @pl.when(has_outer & ~late)
        def _():
            for h in halves:
                relay_grad(s, h).start()
        return carry

    lax.fori_loop(0, S, slot, 0)

    core_copy = pltpu.make_async_remote_copy(gp, p1r, csem.at[0], csem.at[1], **partner)

    def share_rows(q):
        return pl.ds(pl.multiple_of(lax.rem(q, owners) * h3, 8), h3)

    def share_copy(k):
        return pltpu.make_async_remote_copy(
            gp.at[:, share_rows(ring_at(k)), :], p3r.at[k], asem.at[0, k], asem.at[1, k], **ring_peer(k))

    across_copy = pltpu.make_async_remote_copy(p2, p2x, xsem.at[0], xsem.at[1], **across)

    def spread_copy(k, owner):
        rows = share_rows(owner)
        return pltpu.make_async_remote_copy(
            pnew.at[:, rows, :], pnew.at[:, rows, :], agsem.at[0, k], agsem.at[1, k], **ring_peer(k))

    def hand_copy(owner):
        q = lax.rem(owner, owners)
        rows = share_rows(owner)
        return pltpu.make_async_remote_copy(
            pnew.at[:, rows, :], pnew.at[:, rows, :], casem.at[0, q], casem.at[1, q], **partner)

    def source(k):
        return lax.rem(me + ring - k, ring)

    def pass_on(h):
        @pl.when(has_relay)
        def _():
            for s in range(S):
                relay_grad(s, h).wait_recv()
                forward_grad(s, h).start()

    @pl.when(~late)
    def _():
        core_copy.start()

    @pl.when(late)
    def _():
        core_copy.wait_recv()
        gp[...] += p1r[...]
        for k in range(1, ring):
            @pl.when(ring_at(k) < owners)
            def _():
                share_copy(k).start()

        pass_on(halves[0])

        @pl.when(me < owners)
        def _():
            total = gp[:, share_rows(me), :]
            for k in range(1, ring):
                share_copy(k).wait_recv()
                total = total + p3r[k]
            p2[...] = total
            across_copy.start()

        @pl.when(has_outer)
        def _():
            for s in range(S):
                outer_grad(s, halves[1]).start()
        pass_on(halves[1])

    def covers(block, r):
        rows = lax.broadcasted_iota(jnp.int32, (HALO, HALO), 0) + (block * HALO - r)
        return (rows >= 0) & (rows < M)

    def own(totals, block, h):
        for s in range(S):
            inside = covers(block, row_of(s))
            totals = [t + jnp.where(inside, gmid[s, h, c], 0.0) for c, t in enumerate(totals)]
        return totals

    def others(totals, block, h, d):
        for s in range(S):
            inside = covers(block, cor_smem[d, s, 0])
            totals = [t + jnp.where(inside, grecv[d, s, h, c], 0.0) for c, t in enumerate(totals)]
        return totals

    zeros = [jnp.zeros((HALO, HALO), jnp.float32)] * 2

    for s in range(S):
        for h in range(2):
            grad_to(core, s, h, partner).wait_recv()

    def near(block, carry):
        h = lax.rem(block, 2)
        totals = others(own(zeros, block, h), block, h, core)
        rows = pl.ds(pl.multiple_of(block * HALO, HALO), HALO)
        for c in range(2):
            obj_out[c, pl.ds(pl.multiple_of(block * HALO - HALO, HALO), HALO), :] = (
                ext[c, rows, :] - STEP_OBJECT * totals[c])
        return carry

    lax.fori_loop(1, blocks - 1, near, 0)

    @pl.when(late & (me < owners))
    def _():
        live = counts[0]
        for i in range(1, G * PN):
            live = live + counts[i]
        across_copy.wait_recv()
        total = p2[...] + p2x[...]
        divisor = jnp.full(total.shape, live, jnp.int32).astype(jnp.float32)
        pnew[:, share_rows(me), :] = prb[:, share_rows(me), :] - STEP_PROBE * total / divisor
        for k in range(1, ring):
            spread_copy(k, me).start()
        hand_copy(me).start()

    def rim_copy(d):
        return pltpu.make_async_remote_copy(rim.at[d], yrecv.at[d], ysem.at[0, d], ysem.at[1, d], **row_peer[d])

    def finish(h):
        @pl.when(has_outer)
        def _():
            for s in range(S):
                grad_to(1 - core, s, h, partner).wait_recv()
        for d in range(2):
            block = d * (blocks - 1)

            @pl.when(row_send[d] & (h == d))
            def _():
                totals = others(own(zeros, block, d), block, d, core)
                for c in range(2):
                    rim[d, c] = totals[c]

                @pl.when(has_outer)
                def _():
                    more = others([rim[d, c] for c in range(2)], block, d, 1 - core)
                    for c in range(2):
                        rim[d, c] = more[c]
                rim_copy(d).start()

        @pl.when(has_outer)
        def _():
            def far(i, carry):
                block = 2 * i + 2 - h
                totals = others(zeros, block, h, 1 - core)
                rows = pl.ds(pl.multiple_of(block * HALO - HALO, HALO), HALO)
                for c in range(2):
                    obj_out[c, rows, :] = obj_out[c, rows, :] - STEP_OBJECT * totals[c]
                return carry

            lax.fori_loop(0, blocks // 2 - 1, far, 0)

    finish(halves[0])

    @pl.when(late)
    def _():
        for k in range(1, ring):
            @pl.when(source(k) < owners)
            def _():
                spread_copy(k, source(k)).wait_recv()
                hand_copy(source(k)).start()

    finish(halves[1])
    for d in range(2):
        @pl.when(row_recv[d])
        def _():
            rim_copy(d).wait_recv()
            rows = pl.ds((TR - HALO, 0)[d], HALO)
            obj_out[:, rows, :] = obj_out[:, rows, :] - STEP_OBJECT * yrecv[d]

    @pl.when(~late)
    def _():
        for q in range(owners):
            hand_copy(q).wait_recv()
    prb_out[...] = pnew[...]

    for d in range(2):
        @pl.when(col_send[d])
        def _():
            cor_copy(d).wait_send()
            for s in range(S):
                patch_copy(d, s).wait_send()

        @pl.when(row_send[d])
        def _():
            halo_copy(d).wait_send()
            rim_copy(d).wait_send()
    for s in range(S):
        for h in range(2):
            chip_grad(s, h).wait_send()

            @pl.when(has_outer)
            def _():
                outer_grad(s, h).wait_send()

            @pl.when(has_relay)
            def _():
                forward_grad(s, h).wait_send()

    @pl.when(~late)
    def _():
        core_copy.wait_send()

    @pl.when(late)
    def _():
        for k in range(1, ring):
            @pl.when(ring_at(k) < owners)
            def _():
                share_copy(k).wait_send()

        @pl.when(me < owners)
        def _():
            across_copy.wait_send()
            for k in range(1, ring):
                spread_copy(k, me).wait_send()
        for q in range(owners):
            hand_copy(q).wait_send()


def on_device(grp_size, pos_size, tables, object_field, probe_field, patterns, corners, counts):
    TR, S, M = object_field.shape[1], patterns.shape[0], probe_field.shape[1]
    ring = grp_size * (pos_size // 4)
    owners, h3 = shares(M, ring)
    f32 = jnp.float32
    V, D = pltpu.VMEM, pltpu.SemaphoreType.DMA
    smem = pl.BlockSpec(memory_space=pltpu.SMEM)
    hbm = pl.BlockSpec(memory_space=pl.ANY)
    vmem = pl.BlockSpec(memory_space=pltpu.VMEM)
    half = (2, HALO, HALO)
    return pl.pallas_call(
        functools.partial(kernel, (grp_size, pos_size, S, TR, M)),
        out_shape=(
            pltpu.VMEM(object_field.shape, f32),
            pltpu.VMEM(probe_field.shape, f32),
        ),
        in_specs=[smem, smem, hbm, hbm, hbm, hbm],
        out_specs=(vmem, vmem),
        scratch_shapes=[
            V((2, TR + 2 * HALO, HALO), f32),
            V((2, M, M), f32),
            V((2, S, M, HALO), f32),
            V((S, M, M), f32),
            V(tables.shape, jnp.bfloat16),
            V((2, S, 2, M, HALO), f32),
            V((2, S, 2, M, HALO), f32),
            V((8, 128), jnp.int32),
            V((2, 8, 128), jnp.int32),
            pltpu.SMEM((2, 8, 128), jnp.int32),
            V((S, 2, *half), f32),
            V((2, S, 2, *half), f32),
            V((2, S, 2, *half), f32),
            V((S, 2, *half), f32),
            V((2, 2, 2 * M, HALO), f32),
            V((2, *half), f32),
            V((2, *half), f32),
            V((2, M, M), f32),
            V((2, M, M), f32),
            V((ring, 2, h3, M), f32),
            V((2, h3, M), f32),
            V((2, h3, M), f32),
            V((2, M, M), f32),
            D((5,)), D((2, 2)), D((2, 2)), D((2,)), D((2, 2, S)), D((2, 2, S, 2)), D((S, 2)), D((S, 2)), D((2, 2)),
            D((2,)), D((2, ring)), D((2, ring)), D((2,)), D((2, owners)),
        ],
        compiler_params=pltpu.CompilerParams(
            collective_id=0, has_side_effects=True, vmem_limit_bytes=56 * 1024 * 1024
        ),
    )(corners, counts, object_field, probe_field, patterns, jnp.asarray(tables))

def solution(mesh):
    def body(object_field, probe_field, patterns, corners, counts):
        tables = dft_tables(probe_field.shape[1])
        return on_device(
            mesh.shape["grp"], mesh.shape["pos"], tables, object_field, probe_field, patterns, corners, counts
        )

    return jax.shard_map(
        body,
        mesh=mesh,
        in_specs=(
            P(None, "grp", "pos"),
            P(),
            P(("grp", "pos"), None, None),
            P(None, ("grp", "pos")),
            P(),
        ),
        out_specs=(P(None, "grp", "pos"), P()),
        check_vma=False,
    )
```

time: 62.2 us -> 53 us (0.85)
  Pallas kernels: 59.1 us -> 50.4 us
    pallas_call x1, Pallas kernels: 59.1 us -> 50.4 us  [on_device(): pl.pallas_call(functools.partial(kernel, (grp_size, pos_size, S, TR, M)),...]
where the time goes in v2:
time: 53 us; the launch traced here: 52.8 us
  Pallas kernels  50.4 us (95%)
  local copies, waits for them, and re-layouts  1.77 us (3%)
  between operations  0.64 us (1%)
    pallas_call x1, Pallas kernels, on_device(): pl.pallas_call(functools.partial(kernel, (grp_size, pos_size, S, TR, M)),...  50.4 us
    unnamed x2, local copies, waits for them, and re-layouts  1.77 us

profile of v2, /device:TPU:0, one launch (start us, length us, event | category | flops | bytes accessed | tf_op | source)
XLA Modules:
  0.0 52.8 jit_solution(17242004800359053239)
XLA Ops:
  0.6 50.4 %shard_map.77 = (f32[2,1024,128]{2,1,0:T(8,128)S(1)}, f32[2,256,256]{2,1,0:T(8,128)S(1)}) custom-call(s32[2,3]{1,0:T(2,128)} %corners.1, s32[32]{0:T(128)} %counts.1, f32[2,1024,128]{2,1,0:T(8,128)} %obj_hbm.1, f32[2,256,256]{2,1,0:T(8,128)} %prb_hbm.1, f32[3,256,256]{2,1,0:T(8,128)} %pat_hbm.1, bf16[2,2,2,256,256]{4,3,2,1,0:T(8,128)(2,1)} %constant.2.clone.tab_hbm), custom_call_target="tpu_custom_call" | custom-call | tf_op jit(solution)/shard_map/pallas_call | solution.py:533
  51.0 1.0 %copy.10 = f32[2,1024,128]{2,1,0:T(8,128)} copy(f32[2,1024,128]{2,1,0:T(8,128)S(1)} %get-tuple-element.2) | data formatting | bytes 2097152
  52.0 0.8 %copy.11 = f32[2,256,256]{2,1,0:T(8,128)} copy(f32[2,256,256]{2,1,0:T(8,128)S(1)} %get-tuple-element.3) | data formatting | bytes 1048576

commit v3 on v2

--- a/solution.py
+++ b/solution.py
@@ -98,9 +98,9 @@
 
 
 def kernel(sizes, corners, counts, obj_hbm, prb_hbm, pat_hbm, tab_hbm, obj_out, prb_out,
-           ext, prb, pat, patp, tab, nb, stage, corv, cor_recv, cor_smem,
+           ext, prb, pat, patp, tab, nb, stage, cor_smem,
            gmid, gsend, grecv, relay, turned, rim, yrecv, gp, p1r, p3r, p2, p2x, pnew,
-           loc, yh, corsem, cors, patsem, gsem, rsem, fsem, ysem, csem, asem, agsem, xsem, casem):
+           loc, farsem, yh, corsem, patsem, gsem, rsem, fsem, ysem, csem, asem, agsem, xsem, casem):
     G, PN, S, TR, M = sizes
     grp, pos = lax.axis_index("grp"), lax.axis_index("pos")
     core, chip, chips = lax.rem(pos, 2), pos // 2, PN // 2
@@ -143,6 +143,10 @@
     for c in locals_:
         c.start()
 
+    near_ring = [
+        (late & row_send[0], row_peer[0]), (late & row_send[1], row_peer[1]),
+        (late & (pos >= 4), at(grp, pos - 4)), (late & (pos + 4 < PN), at(grp, pos + 4)),
+    ]
     barrier = pltpu.get_barrier_semaphore()
 
     def greet(condition, peers):
@@ -153,30 +157,26 @@
         return condition.astype(jnp.int32) * len(peers)
 
     expected = greet(col_send[0], [col_peer[0]]) + greet(col_send[1], [col_peer[1]])
-    expected += greet(~late & row_send[0], [row_peer[0]]) + greet(~late & row_send[1], [row_peer[1]])
-    expected += greet(late, [ring_peer(k) for k in range(1, ring)])
+    expected += greet(row_send[0], [row_peer[0]]) + greet(row_send[1], [row_peer[1]])
+    expected += greet(near_ring[2][0], [near_ring[2][1]]) + greet(near_ring[3][0], [near_ring[3][1]])
     expected += greet(~late & has_outer, [relay_peer, feeder]) + greet(has_relay, [relay_peer, forward_peer])
 
     lane = lax.broadcasted_iota(jnp.int32, (M, HALO), 1)
-    row8 = lax.broadcasted_iota(jnp.int32, (8, 128), 0)
-    packed = jnp.zeros((8, 128), jnp.int32)
-    for s in range(S):
-        packed = jnp.where(row8 == s, corners[0, s] - grp * TR + HALO, packed)
-    corv[...] = packed
     gp[...] = jnp.zeros(gp.shape, jnp.float32)
 
+    locals_[0].wait()
     pl.semaphore_wait(barrier, expected)
 
     def cor_copy(d):
-        return pltpu.make_async_remote_copy(corv, cor_recv.at[d], corsem.at[0, d], corsem.at[1, d], **col_peer[d])
-
-    def cor_local(d):
-        return pltpu.make_async_copy(cor_recv.at[d], cor_smem.at[d], cors.at[d])
+        return pltpu.make_async_remote_copy(corners, cor_smem.at[d], corsem.at[0, d], corsem.at[1, d], **col_peer[d])
+
+    def row_at(d, s):
+        return jnp.clip(cor_smem[d, 0, s] - grp * TR + HALO, 0, TR + 2 * HALO - M)
 
     def halo_copy(d):
-        src, dst = ((0, HALO + TR), (TR - HALO, 0))[d]
-        return pltpu.make_async_remote_copy(
-            obj_hbm.at[:, pl.ds(src, HALO), :], ext.at[:, pl.ds(dst, HALO), :], yh.at[0, d], yh.at[1, d], **row_peer[d])
+        src, dst = ((HALO, HALO + TR), (TR, 0))[d]
+        return pltpu.make_async_remote_copy(
+            ext.at[:, pl.ds(src, HALO), :], ext.at[:, pl.ds(dst, HALO), :], yh.at[0, d], yh.at[1, d], **row_peer[d])
 
     for d in range(2):
         @pl.when(col_send[d])
@@ -190,12 +190,6 @@
         @pl.when(col_recv[d])
         def _():
             cor_copy(d).wait_recv()
-            cor_local(d).start()
-    for d in range(2):
-        @pl.when(col_recv[d])
-        def _():
-            cor_local(d).wait()
-    locals_[0].wait()
     for d in range(2):
         @pl.when(row_recv[d])
         def _():
@@ -209,10 +203,21 @@
         for d in range(2):
             @pl.when(col_send[d])
             def _():
-                r = jnp.clip(cor_smem[1 - d, s, 0], 0, TR + 2 * HALO - M)
+                r = row_at(1 - d, s)
                 for c in range(2):
                     stage[d, s, c] = ext[c, pl.ds(r, M), :]
                 patch_copy(d, s).start()
+
+    for step in range(lines + G - 3):
+        for there, peer in near_ring:
+            @pl.when(there)
+            def _():
+                pl.semaphore_signal(farsem.at[step], inc=1, **peer)
+        known = sum(there.astype(jnp.int32) for there, _ in near_ring)
+
+        @pl.when(late)
+        def _():
+            pl.semaphore_wait(farsem.at[step], known)
 
     def grad_to(d, s, h, peer):
         return pltpu.make_async_remote_copy(
@@ -303,8 +308,7 @@
 
         @pl.when(has_outer & ~late)
         def _():
-            for h in halves:
-                relay_grad(s, h).start()
+            relay_grad(s, halves[0]).start()
         return carry
 
     lax.fori_loop(0, S, slot, 0)
@@ -314,22 +318,23 @@
     def share_rows(q):
         return pl.ds(pl.multiple_of(lax.rem(q, owners) * h3, 8), h3)
 
-    def share_copy(k):
-        return pltpu.make_async_remote_copy(
-            gp.at[:, share_rows(ring_at(k)), :], p3r.at[k], asem.at[0, k], asem.at[1, k], **ring_peer(k))
-
-    across_copy = pltpu.make_async_remote_copy(p2, p2x, xsem.at[0], xsem.at[1], **across)
-
-    def spread_copy(k, owner):
+    def share_copy(c, k):
+        return pltpu.make_async_remote_copy(
+            gp.at[c, share_rows(ring_at(k)), :], p3r.at[c, k], asem.at[0, c, k], asem.at[1, c, k], **ring_peer(k))
+
+    def across_copy(c):
+        return pltpu.make_async_remote_copy(p2.at[c], p2x.at[c], xsem.at[0, c], xsem.at[1, c], **across)
+
+    def spread_copy(c, k, owner):
         rows = share_rows(owner)
         return pltpu.make_async_remote_copy(
-            pnew.at[:, rows, :], pnew.at[:, rows, :], agsem.at[0, k], agsem.at[1, k], **ring_peer(k))
-
-    def hand_copy(owner):
+            pnew.at[c, rows, :], pnew.at[c, rows, :], agsem.at[0, c, k], agsem.at[1, c, k], **ring_peer(k))
+
+    def hand_copy(c, owner):
         q = lax.rem(owner, owners)
         rows = share_rows(owner)
         return pltpu.make_async_remote_copy(
-            pnew.at[:, rows, :], pnew.at[:, rows, :], casem.at[0, q], casem.at[1, q], **partner)
+            pnew.at[c, rows, :], pnew.at[c, rows, :], casem.at[0, c, q], casem.at[1, c, q], **partner)
 
     def source(k):
         return lax.rem(me + ring - k, ring)
@@ -340,36 +345,6 @@
             for s in range(S):
                 relay_grad(s, h).wait_recv()
                 forward_grad(s, h).start()
-
-    @pl.when(~late)
-    def _():
-        core_copy.start()
-
-    @pl.when(late)
-    def _():
-        core_copy.wait_recv()
-        gp[...] += p1r[...]
-        for k in range(1, ring):
-            @pl.when(ring_at(k) < owners)
-            def _():
-                share_copy(k).start()
-
-        pass_on(halves[0])
-
-        @pl.when(me < owners)
-        def _():
-            total = gp[:, share_rows(me), :]
-            for k in range(1, ring):
-                share_copy(k).wait_recv()
-                total = total + p3r[k]
-            p2[...] = total
-            across_copy.start()
-
-        @pl.when(has_outer)
-        def _():
-            for s in range(S):
-                outer_grad(s, halves[1]).start()
-        pass_on(halves[1])
 
     def covers(block, r):
         rows = lax.broadcasted_iota(jnp.int32, (HALO, HALO), 0) + (block * HALO - r)
@@ -383,15 +358,11 @@
 
     def others(totals, block, h, d):
         for s in range(S):
-            inside = covers(block, cor_smem[d, s, 0])
+            inside = covers(block, row_at(d, s))
             totals = [t + jnp.where(inside, grecv[d, s, h, c], 0.0) for c, t in enumerate(totals)]
         return totals
 
     zeros = [jnp.zeros((HALO, HALO), jnp.float32)] * 2
-
-    for s in range(S):
-        for h in range(2):
-            grad_to(core, s, h, partner).wait_recv()
 
     def near(block, carry):
         h = lax.rem(block, 2)
@@ -402,20 +373,67 @@
                 ext[c, rows, :] - STEP_OBJECT * totals[c])
         return carry
 
-    lax.fori_loop(1, blocks - 1, near, 0)
-
-    @pl.when(late & (me < owners))
+    def near_all():
+        for s in range(S):
+            for h in range(2):
+                grad_to(core, s, h, partner).wait_recv()
+        lax.fori_loop(1, blocks - 1, near, 0)
+
+    def second(first, last):
+        @pl.when(has_outer)
+        def _():
+            for s in range(first, last):
+                outer_grad(s, halves[1]).start()
+
+    @pl.when(~late)
     def _():
+        core_copy.start()
+
+        @pl.when(has_outer)
+        def _():
+            for s in range(S):
+                relay_grad(s, halves[1]).start()
+        near_all()
+
+    @pl.when(late)
+    def _():
+        core_copy.wait_recv()
+        gp[...] += p1r[...]
+        for c in range(2):
+            for k in range(1, ring):
+                @pl.when(ring_at(k) < owners)
+                def _():
+                    share_copy(c, k).start()
+
+        pass_on(halves[0])
+        near_all()
+        for c in range(2):
+            @pl.when(me < owners)
+            def _():
+                total = gp[c, share_rows(me), :]
+                for k in range(1, ring):
+                    share_copy(c, k).wait_recv()
+                    total = total + p3r[c, k]
+                p2[c] = total
+                across_copy(c).start()
+
+            second(*((0, 1), (1, S))[c])
+
+        pass_on(halves[1])
         live = counts[0]
         for i in range(1, G * PN):
             live = live + counts[i]
-        across_copy.wait_recv()
-        total = p2[...] + p2x[...]
-        divisor = jnp.full(total.shape, live, jnp.int32).astype(jnp.float32)
-        pnew[:, share_rows(me), :] = prb[:, share_rows(me), :] - STEP_PROBE * total / divisor
-        for k in range(1, ring):
-            spread_copy(k, me).start()
-        hand_copy(me).start()
+
+        @pl.when(me < owners)
+        def _():
+            for c in range(2):
+                across_copy(c).wait_recv()
+                total = p2[c] + p2x[c]
+                divisor = jnp.full(total.shape, live, jnp.int32).astype(jnp.float32)
+                pnew[c, share_rows(me), :] = prb[c, share_rows(me), :] - STEP_PROBE * total / divisor
+                for k in range(1, ring):
+                    spread_copy(c, k, me).start()
+                hand_copy(c, me).start()
 
     def rim_copy(d):
         return pltpu.make_async_remote_copy(rim.at[d], yrecv.at[d], ysem.at[0, d], ysem.at[1, d], **row_peer[d])
@@ -457,11 +475,12 @@
 
     @pl.when(late)
     def _():
-        for k in range(1, ring):
-            @pl.when(source(k) < owners)
-            def _():
-                spread_copy(k, source(k)).wait_recv()
-                hand_copy(source(k)).start()
+        for c in range(2):
+            for k in range(1, ring):
+                @pl.when(source(k) < owners)
+                def _():
+                    spread_copy(c, k, source(k)).wait_recv()
+                    hand_copy(c, source(k)).start()
 
     finish(halves[1])
     for d in range(2):
@@ -473,8 +492,9 @@
 
     @pl.when(~late)
     def _():
-        for q in range(owners):
-            hand_copy(q).wait_recv()
+        for c in range(2):
+            for q in range(owners):
+                hand_copy(c, q).wait_recv()
     prb_out[...] = pnew[...]
 
     for d in range(2):
@@ -506,18 +526,19 @@
 
     @pl.when(late)
     def _():
-        for k in range(1, ring):
-            @pl.when(ring_at(k) < owners)
-            def _():
-                share_copy(k).wait_send()
-
-        @pl.when(me < owners)
-        def _():
-            across_copy.wait_send()
+        for c in range(2):
             for k in range(1, ring):
-                spread_copy(k, me).wait_send()
-        for q in range(owners):
-            hand_copy(q).wait_send()
+                @pl.when(ring_at(k) < owners)
+                def _():
+                    share_copy(c, k).wait_send()
+
+            @pl.when(me < owners)
+            def _():
+                across_copy(c).wait_send()
+                for k in range(1, ring):
+                    spread_copy(c, k, me).wait_send()
+            for q in range(owners):
+                hand_copy(c, q).wait_send()
 
 
 def on_device(grp_size, pos_size, tables, object_field, probe_field, patterns, corners, counts):
@@ -546,9 +567,7 @@
             V(tables.shape, jnp.bfloat16),
             V((2, S, 2, M, HALO), f32),
             V((2, S, 2, M, HALO), f32),
-            V((8, 128), jnp.int32),
-            V((2, 8, 128), jnp.int32),
-            pltpu.SMEM((2, 8, 128), jnp.int32),
+            pltpu.SMEM((2, *corners.shape), jnp.int32),
             V((S, 2, *half), f32),
             V((2, S, 2, *half), f32),
             V((2, S, 2, *half), f32),
@@ -558,12 +577,12 @@
             V((2, *half), f32),
             V((2, M, M), f32),
             V((2, M, M), f32),
-            V((ring, 2, h3, M), f32),
+            V((2, ring, h3, M), f32),
             V((2, h3, M), f32),
             V((2, h3, M), f32),
             V((2, M, M), f32),
-            D((5,)), D((2, 2)), D((2, 2)), D((2,)), D((2, 2, S)), D((2, 2, S, 2)), D((S, 2)), D((S, 2)), D((2, 2)),
-            D((2,)), D((2, ring)), D((2, ring)), D((2,)), D((2, owners)),
+            D((5,)), pltpu.SemaphoreType.REGULAR((max(1, grp_size + pos_size // 4 - 3),)), D((2, 2)), D((2, 2)), D((2, 2, S)), D((2, 2, S, 2)), D((S, 2)), D((S, 2)), D((2, 2)),
+            D((2,)), D((2, 2, ring)), D((2, 2, ring)), D((2, 2)), D((2, 2, owners)),
         ],
         compiler_params=pltpu.CompilerParams(
             collective_id=0, has_side_effects=True, vmem_limit_bytes=56 * 1024 * 1024

time: 53 us -> 51.1 us (0.964)
  Pallas kernels: 50.4 us -> 48.6 us
    pallas_call x1, Pallas kernels: 50.4 us -> 48.6 us  [on_device(): pl.pallas_call(functools.partial(kernel, (grp_size, pos_size, S, TR, M)),...]
where the time goes in v3:
time: 51.1 us; the launch traced here: 51 us
  Pallas kernels  48.6 us (95%)
  local copies, waits for them, and re-layouts  1.77 us (3%)
  between operations  0.64 us (1%)
    pallas_call x1, Pallas kernels, on_device(): pl.pallas_call(functools.partial(kernel, (grp_size, pos_size, S, TR, M)),...  48.6 us
    unnamed x2, local copies, waits for them, and re-layouts  1.77 us

profile of v3, /device:TPU:0, one launch (start us, length us, event | category | flops | bytes accessed | tf_op | source)
XLA Modules:
  0.0 51.0 jit_solution(12526102170704612102)
XLA Ops:
  0.6 48.6 %shard_map.77 = (f32[2,1024,128]{2,1,0:T(8,128)S(1)}, f32[2,256,256]{2,1,0:T(8,128)S(1)}) custom-call(s32[2,3]{1,0:T(2,128)} %corners.1, s32[32]{0:T(128)} %counts.1, f32[2,1024,128]{2,1,0:T(8,128)} %obj_hbm.1, f32[2,256,256]{2,1,0:T(8,128)} %prb_hbm.1, f32[3,256,256]{2,1,0:T(8,128)} %pat_hbm.1, bf16[2,2,2,256,256]{4,3,2,1,0:T(8,128)(2,1)} %constant.2.clone.tab_hbm), custom_call_target="tpu_custom_call" | custom-call | tf_op jit(solution)/shard_map/pallas_call | solution.py:554
  49.2 1.0 %copy.10 = f32[2,1024,128]{2,1,0:T(8,128)} copy(f32[2,1024,128]{2,1,0:T(8,128)S(1)} %get-tuple-element.2) | data formatting | bytes 2097152
  50.2 0.8 %copy.11 = f32[2,256,256]{2,1,0:T(8,128)} copy(f32[2,256,256]{2,1,0:T(8,128)S(1)} %get-tuple-element.3) | data formatting | bytes 1048576

commit v4 on v3

--- a/solution.py
+++ b/solution.py
@@ -92,6 +92,10 @@
     return side_by_side(cols_of(total, 0), cols_of(rest, 0)), side_by_side(cols_of(total, 1), cols_of(rest, 1))
 
 
+def drain(ref, sem):
+    pltpu.make_async_copy(ref, ref, sem).wait()
+
+
 def shares(rows, ring):
     owners = min(ring, rows // 8)
     return owners, rows // owners
@@ -100,7 +104,7 @@
 def kernel(sizes, corners, counts, obj_hbm, prb_hbm, pat_hbm, tab_hbm, obj_out, prb_out,
            ext, prb, pat, patp, tab, nb, stage, cor_smem,
            gmid, gsend, grecv, relay, turned, rim, yrecv, gp, p1r, p3r, p2, p2x, pnew,
-           loc, farsem, yh, corsem, patsem, gsem, rsem, fsem, ysem, csem, asem, agsem, xsem, casem):
+           loc, farsem, yh, corsem, patsem, gsem, rsem, ysem, csem, asem, agsem, xsem, casem, outsem):
     G, PN, S, TR, M = sizes
     grp, pos = lax.axis_index("grp"), lax.axis_index("pos")
     core, chip, chips = lax.rem(pos, 2), pos // 2, PN // 2
@@ -137,7 +141,7 @@
         pltpu.make_async_copy(prb_hbm, prb, loc.at[1]),
         pltpu.make_async_copy(tab_hbm, tab, loc.at[2]),
     ] + [
-        pltpu.make_async_copy(pat_hbm.at[:, :, pl.ds(w * HALO, HALO)], pat.at[w], loc.at[3 + w])
+        pltpu.make_async_copy(pat_hbm.at[:, :, pl.ds(w * HALO, HALO)], pat.at[w], loc.at[3])
         for w in range(2)
     ]
     for c in locals_:
@@ -197,7 +201,7 @@
 
     def patch_copy(d, s):
         return pltpu.make_async_remote_copy(
-            stage.at[d, s], nb.at[d, s], patsem.at[0, d, s], patsem.at[1, d, s], **col_peer[d])
+            stage.at[d, s], nb.at[d, s], outsem.at[d], patsem.at[d, s], **col_peer[d])
 
     for s in range(S):
         for d in range(2):
@@ -219,29 +223,29 @@
         def _():
             pl.semaphore_wait(farsem.at[step], known)
 
-    def grad_to(d, s, h, peer):
-        return pltpu.make_async_remote_copy(
-            gsend.at[d, s, h], grecv.at[d, s, h], gsem.at[0, d, s, h], gsem.at[1, d, s, h], **peer)
-
     def chip_grad(s, h):
-        return grad_to(1 - core, s, h, partner)
+        d = 1 - core
+        return pltpu.make_async_remote_copy(
+            gsend.at[d, h, s], grecv.at[d, h, s], outsem.at[2 + d], gsem.at[d, 0], **partner)
 
     def outer_grad(s, h):
-        return grad_to(core, s, h, across)
+        return pltpu.make_async_remote_copy(
+            gsend.at[core, h, s], grecv.at[core, h, s], outsem.at[2 + core], gsem.at[core, h], **across)
 
     def relay_grad(s, h):
         return pltpu.make_async_remote_copy(
-            gsend.at[core, s, h], relay.at[s, h], gsem.at[0, core, s, h], rsem.at[s, h], **relay_peer)
+            gsend.at[core, h, s], relay.at[h, s], outsem.at[2 + core], rsem.at[h], **relay_peer)
 
     def forward_grad(s, h):
         return pltpu.make_async_remote_copy(
-            relay.at[s, h], grecv.at[1 - core, s, h], fsem.at[s, h], gsem.at[1, 1 - core, s, h], **forward_peer)
+            relay.at[h, s], grecv.at[1 - core, h, s], outsem.at[4], gsem.at[1 - core, h], **forward_peer)
 
     first_half = (grp < G - 1).astype(jnp.int32)
     halves = [first_half, 1 - first_half]
 
-    for c in locals_[1:]:
+    for c in locals_[1:3]:
         c.wait()
+    drain(pat, loc.at[3])
     own_count = counts[grp * PN + pos]
 
     column = lax.broadcasted_iota(jnp.int32, (M, M), 1)
@@ -296,9 +300,9 @@
             g0, g1 = [pltpu.roll(turned[c, w, pl.ds(start, M), :], forth, 1) for w in range(2)]
             left, middle, right = jnp.where(tail, g0, 0.0), jnp.where(tail, g1, g0), jnp.where(tail, 0.0, g1)
             for h in range(2):
-                gsend[0, s, h, c] = rows_of(left, h)
+                gsend[0, h, s, c] = rows_of(left, h)
                 gmid[s, h, c] = rows_of(middle, h)
-                gsend[1, s, h, c] = rows_of(right, h)
+                gsend[1, h, s, c] = rows_of(right, h)
         for h in range(2):
             chip_grad(s, h).start()
 
@@ -320,7 +324,7 @@
 
     def share_copy(c, k):
         return pltpu.make_async_remote_copy(
-            gp.at[c, share_rows(ring_at(k)), :], p3r.at[c, k], asem.at[0, c, k], asem.at[1, c, k], **ring_peer(k))
+            gp.at[c, share_rows(ring_at(k)), :], p3r.at[c, k - 1], outsem.at[5], asem.at[c], **ring_peer(k))
 
     def across_copy(c):
         return pltpu.make_async_remote_copy(p2.at[c], p2x.at[c], xsem.at[0, c], xsem.at[1, c], **across)
@@ -328,13 +332,12 @@
     def spread_copy(c, k, owner):
         rows = share_rows(owner)
         return pltpu.make_async_remote_copy(
-            pnew.at[c, rows, :], pnew.at[c, rows, :], agsem.at[0, c, k], agsem.at[1, c, k], **ring_peer(k))
+            pnew.at[c, rows, :], pnew.at[c, rows, :], outsem.at[6], agsem.at[c, k - 1], **ring_peer(k))
 
     def hand_copy(c, owner):
-        q = lax.rem(owner, owners)
         rows = share_rows(owner)
         return pltpu.make_async_remote_copy(
-            pnew.at[c, rows, :], pnew.at[c, rows, :], casem.at[0, c, q], casem.at[1, c, q], **partner)
+            pnew.at[c, rows, :], pnew.at[c, rows, :], outsem.at[7], casem.at[0], **partner)
 
     def source(k):
         return lax.rem(me + ring - k, ring)
@@ -342,8 +345,8 @@
     def pass_on(h):
         @pl.when(has_relay)
         def _():
+            drain(relay.at[h], rsem.at[h])
             for s in range(S):
-                relay_grad(s, h).wait_recv()
                 forward_grad(s, h).start()
 
     def covers(block, r):
@@ -359,7 +362,7 @@
     def others(totals, block, h, d):
         for s in range(S):
             inside = covers(block, row_at(d, s))
-            totals = [t + jnp.where(inside, grecv[d, s, h, c], 0.0) for c, t in enumerate(totals)]
+            totals = [t + jnp.where(inside, grecv[d, h, s, c], 0.0) for c, t in enumerate(totals)]
         return totals
 
     zeros = [jnp.zeros((HALO, HALO), jnp.float32)] * 2
@@ -374,9 +377,7 @@
         return carry
 
     def near_all():
-        for s in range(S):
-            for h in range(2):
-                grad_to(core, s, h, partner).wait_recv()
+        drain(grecv.at[core], gsem.at[core, 0])
         lax.fori_loop(1, blocks - 1, near, 0)
 
     def second(first, last):
@@ -411,8 +412,8 @@
             @pl.when(me < owners)
             def _():
                 total = gp[c, share_rows(me), :]
-                for k in range(1, ring):
-                    share_copy(c, k).wait_recv()
+                drain(p3r.at[c], asem.at[c])
+                for k in range(ring - 1):
                     total = total + p3r[c, k]
                 p2[c] = total
                 across_copy(c).start()
@@ -441,8 +442,7 @@
     def finish(h):
         @pl.when(has_outer)
         def _():
-            for s in range(S):
-                grad_to(1 - core, s, h, partner).wait_recv()
+            drain(grecv.at[1 - core, h], gsem.at[1 - core, h])
         for d in range(2):
             block = d * (blocks - 1)
 
@@ -492,33 +492,28 @@
 
     @pl.when(~late)
     def _():
-        for c in range(2):
-            for q in range(owners):
-                hand_copy(c, q).wait_recv()
+        drain(pnew, casem.at[0])
     prb_out[...] = pnew[...]
 
     for d in range(2):
         @pl.when(col_send[d])
         def _():
             cor_copy(d).wait_send()
-            for s in range(S):
-                patch_copy(d, s).wait_send()
+            drain(stage.at[d], outsem.at[d])
 
         @pl.when(row_send[d])
         def _():
             halo_copy(d).wait_send()
             rim_copy(d).wait_send()
-    for s in range(S):
-        for h in range(2):
-            chip_grad(s, h).wait_send()
-
-            @pl.when(has_outer)
-            def _():
-                outer_grad(s, h).wait_send()
-
-            @pl.when(has_relay)
-            def _():
-                forward_grad(s, h).wait_send()
+    drain(gsend.at[1 - core], outsem.at[3 - core])
+
+    @pl.when(has_outer)
+    def _():
+        drain(gsend.at[core], outsem.at[2 + core])
+
+    @pl.when(has_relay)
+    def _():
+        drain(relay, outsem.at[4])
 
     @pl.when(~late)
     def _():
@@ -526,19 +521,35 @@
 
     @pl.when(late)
     def _():
-        for c in range(2):
-            for k in range(1, ring):
-                @pl.when(ring_at(k) < owners)
+        if ring == owners:
+            drain(p3r, outsem.at[5])
+            drain(p3r, outsem.at[6])
+        else:
+            for c in range(2):
+                for k in range(1, ring):
+                    @pl.when(ring_at(k) < owners)
+                    def _():
+                        share_copy(c, k).wait_send()
+
+                @pl.when(me < owners)
                 def _():
-                    share_copy(c, k).wait_send()
-
-            @pl.when(me < owners)
-            def _():
+                    for k in range(1, ring):
+                        spread_copy(c, k, me).wait_send()
+
+        @pl.when(me < owners)
+        def _():
+            for c in range(2):
                 across_copy(c).wait_send()
-                for k in range(1, ring):
-                    spread_copy(c, k, me).wait_send()
-            for q in range(owners):
-                hand_copy(c, q).wait_send()
+        drain(pnew, outsem.at[7])
+
+
+def store(obj, prb, obj_out, prb_out, sems):
+    copies = [pltpu.make_async_copy(obj.at[c], obj_out.at[c], sems.at[c]) for c in range(2)]
+    copies.append(pltpu.make_async_copy(prb, prb_out, sems.at[2]))
+    for c in copies:
+        c.start()
+    for c in copies:
+        c.wait()
 
 
 def on_device(grp_size, pos_size, tables, object_field, probe_field, patterns, corners, counts):
@@ -551,7 +562,7 @@
     hbm = pl.BlockSpec(memory_space=pl.ANY)
     vmem = pl.BlockSpec(memory_space=pltpu.VMEM)
     half = (2, HALO, HALO)
-    return pl.pallas_call(
+    object_new, probe_new = pl.pallas_call(
         functools.partial(kernel, (grp_size, pos_size, S, TR, M)),
         out_shape=(
             pltpu.VMEM(object_field.shape, f32),
@@ -569,25 +580,38 @@
             V((2, S, 2, M, HALO), f32),
             pltpu.SMEM((2, *corners.shape), jnp.int32),
             V((S, 2, *half), f32),
-            V((2, S, 2, *half), f32),
-            V((2, S, 2, *half), f32),
-            V((S, 2, *half), f32),
+            V((2, 2, S, *half), f32),
+            V((2, 2, S, *half), f32),
+            V((2, S, *half), f32),
             V((2, 2, 2 * M, HALO), f32),
             V((2, *half), f32),
             V((2, *half), f32),
             V((2, M, M), f32),
             V((2, M, M), f32),
-            V((2, ring, h3, M), f32),
+            V((2, ring - 1, h3, M), f32),
             V((2, h3, M), f32),
             V((2, h3, M), f32),
             V((2, M, M), f32),
-            D((5,)), pltpu.SemaphoreType.REGULAR((max(1, grp_size + pos_size // 4 - 3),)), D((2, 2)), D((2, 2)), D((2, 2, S)), D((2, 2, S, 2)), D((S, 2)), D((S, 2)), D((2, 2)),
-            D((2,)), D((2, 2, ring)), D((2, 2, ring)), D((2, 2)), D((2, 2, owners)),
+            D((4,)), pltpu.SemaphoreType.REGULAR((max(1, grp_size + pos_size // 4 - 3),)), D((2, 2)), D((2, 2)), D((2, S)),
+            D((2, 2)), D((2,)), D((2, 2)), D((2,)), D((2,)), D((2, ring - 1)), D((2, 2)), D((1,)), D((8,)),
         ],
         compiler_params=pltpu.CompilerParams(
             collective_id=0, has_side_effects=True, vmem_limit_bytes=56 * 1024 * 1024
         ),
     )(corners, counts, object_field, probe_field, patterns, jnp.asarray(tables))
+    object_new = pltpu.with_memory_space_constraint(object_new, pltpu.VMEM)
+    probe_new = pltpu.with_memory_space_constraint(probe_new, pltpu.VMEM)
+    return pl.pallas_call(
+        store,
+        out_shape=(
+            jax.ShapeDtypeStruct(object_field.shape, f32),
+            jax.ShapeDtypeStruct(probe_field.shape, f32),
+        ),
+        in_specs=[hbm, hbm],
+        out_specs=(hbm, hbm),
+        scratch_shapes=[D((3,))],
+        compiler_params=pltpu.CompilerParams(vmem_limit_bytes=1024 * 1024),
+    )(object_new, probe_new)
 
 def solution(mesh):
     def body(object_field, probe_field, patterns, corners, counts):

time: 51.1 us -> 49.5 us (0.969)
  local copies, waits for them, and re-layouts: 1.77 us -> 0 us
    unnamed x2 -> x0, local copies, waits for them, and re-layouts: 1.77 us -> none
    pallas_call x0 -> x1, Pallas kernels: none -> 1.17 us  [on_device(): pl.pallas_call(store, out_shape=(jax.ShapeDtypeStruct(object_field.shape,...]
    pallas_call x1, Pallas kernels: 48.6 us -> 47.5 us  [on_device(): pl.pallas_call(functools.partial(kernel, (grp_size, pos_size, S, TR, M)),...]
where the time goes in v4:
time: 49.5 us; the launch traced here: 49.3 us
  Pallas kernels  48.7 us (98%)
  between operations  0.64 us (1%)
    pallas_call x1, Pallas kernels, on_device(): pl.pallas_call(functools.partial(kernel, (grp_size, pos_size, S, TR, M)),...  47.5 us
    pallas_call x1, Pallas kernels, on_device(): pl.pallas_call(store, out_shape=(jax.ShapeDtypeStruct(object_field.shape,...  1.17 us

profile of v4, /device:TPU:0, one launch (start us, length us, event | category | flops | bytes accessed | tf_op | source)
XLA Modules:
  0.0 49.3 jit_solution(1426685685941520549)
XLA Ops:
  0.6 47.5 %shard_map.77 = (f32[2,1024,128]{2,1,0:T(8,128)S(1)}, f32[2,256,256]{2,1,0:T(8,128)S(1)}) custom-call(s32[2,3]{1,0:T(2,128)} %corners.1, s32[32]{0:T(128)} %counts.1, f32[2,1024,128]{2,1,0:T(8,128)} %obj_hbm.1, f32[2,256,256]{2,1,0:T(8,128)} %prb_hbm.1, f32[3,256,256]{2,1,0:T(8,128)} %pat_hbm.1, bf16[2,2,2,256,256]{4,3,2,1,0:T(8,128)(2,1)} %constant.2.clone.tab_hbm), custom_call_target="tpu_custom_call" | custom-call | tf_op jit(solution)/shard_map/pallas_call | solution.py:565
  48.2 1.2 %shard_map.78 = (f32[2,1024,128]{2,1,0:T(8,128)}, f32[2,256,256]{2,1,0:T(8,128)}) custom-call(f32[2,1024,128]{2,1,0:T(8,128)S(1)} %get-tuple-element.4.obj, f32[2,256,256]{2,1,0:T(8,128)S(1)} %get-tuple-element.5.prb), custom_call_target="tpu_custom_call" | custom-call | tf_op jit(solution)/shard_map/pallas_call | solution.py:604

commit v5 on v4

--- a/solution.py
+++ b/solution.py
@@ -101,8 +101,8 @@
     return owners, rows // owners
 
 
-def kernel(sizes, corners, counts, obj_hbm, prb_hbm, pat_hbm, tab_hbm, obj_out, prb_out,
-           ext, prb, pat, patp, tab, nb, stage, cor_smem,
+def kernel(sizes, cor_hbm, cnt_hbm, obj_hbm, prb_hbm, pat_hbm, tab_hbm, obj_out, prb_out,
+           corners, counts, ext, body, prb, prb2, pat, patp, tab, nb, stage, cor_smem,
            gmid, gsend, grecv, relay, turned, rim, yrecv, gp, p1r, p3r, p2, p2x, pnew,
            loc, farsem, yh, corsem, patsem, gsem, rsem, ysem, csem, asem, agsem, xsem, casem, outsem):
     G, PN, S, TR, M = sizes
@@ -137,15 +137,19 @@
         return at(q // lines, (lax.rem(q, lines) * 2 + side) * 2 + core)
 
     locals_ = [
-        pltpu.make_async_copy(obj_hbm, ext.at[:, pl.ds(HALO, TR), :], loc.at[0]),
-        pltpu.make_async_copy(prb_hbm, prb, loc.at[1]),
-        pltpu.make_async_copy(tab_hbm, tab, loc.at[2]),
-    ] + [
-        pltpu.make_async_copy(pat_hbm.at[:, :, pl.ds(w * HALO, HALO)], pat.at[w], loc.at[3])
-        for w in range(2)
+        pltpu.make_async_copy(cor_hbm, corners, loc.at[0]),
+        pltpu.make_async_copy(obj_hbm, body, loc.at[1]),
+        pltpu.make_async_copy(obj_hbm, ext.at[:, pl.ds(HALO, TR), :], loc.at[2]),
+        pltpu.make_async_copy(cnt_hbm, counts, loc.at[3]),
+        pltpu.make_async_copy(prb_hbm, prb, loc.at[4]),
+        pltpu.make_async_copy(tab_hbm, tab, loc.at[5]),
     ]
-    for c in locals_:
-        c.start()
+    for w in range(2):
+        columns = pl.ds(w * HALO, HALO)
+        locals_.append(pltpu.make_async_copy(pat_hbm.at[:, :, columns], pat.at[w], loc.at[6]))
+        for turn in range(2):
+            locals_.append(pltpu.make_async_copy(
+                prb_hbm.at[:, :, columns], prb2.at[:, w, pl.ds(turn * M, M), :], loc.at[7]))
 
     near_ring = [
         (late & row_send[0], row_peer[0]), (late & row_send[1], row_peer[1]),
@@ -165,10 +169,13 @@
     expected += greet(near_ring[2][0], [near_ring[2][1]]) + greet(near_ring[3][0], [near_ring[3][1]])
     expected += greet(~late & has_outer, [relay_peer, feeder]) + greet(has_relay, [relay_peer, forward_peer])
 
+    for c in locals_:
+        c.start()
     lane = lax.broadcasted_iota(jnp.int32, (M, HALO), 1)
     gp[...] = jnp.zeros(gp.shape, jnp.float32)
 
-    locals_[0].wait()
+    for c in locals_[:3]:
+        c.wait()
     pl.semaphore_wait(barrier, expected)
 
     def cor_copy(d):
@@ -194,23 +201,44 @@
         @pl.when(col_recv[d])
         def _():
             cor_copy(d).wait_recv()
-    for d in range(2):
-        @pl.when(row_recv[d])
-        def _():
-            halo_copy(d).wait_recv()
-
-    def patch_copy(d, s):
-        return pltpu.make_async_remote_copy(
-            stage.at[d, s], nb.at[d, s], outsem.at[d], patsem.at[d, s], **col_peer[d])
-
-    for s in range(S):
+    first_half = (grp < G - 1).astype(jnp.int32)
+    halves = [first_half, 1 - first_half]
+
+    def patch_copy(d, s, h):
+        return pltpu.make_async_remote_copy(
+            stage.at[d, s, h], nb.at[d, s, h], outsem.at[d], patsem.at[d, s], **col_peer[d])
+
+    def wrapped(source, inset, c, r, h):
+        after = r + HALO * (1 - h)
+        base = after - lax.rem(after, 2 * HALO) + HALO * h
+        last = source.shape[1] - HALO
+        low, high = [
+            source[c, pl.ds(jnp.clip(at_row - inset * HALO, 0, last), HALO), :]
+            for at_row in (base, base + 2 * HALO)
+        ]
+        rows = lax.broadcasted_iota(jnp.int32, (HALO, HALO), 0) + base
+        return jnp.where(rows >= r, low, high)
+
+    def send_patch(s, which):
+        h = halves[which]
         for d in range(2):
             @pl.when(col_send[d])
             def _():
                 r = row_at(1 - d, s)
                 for c in range(2):
-                    stage[d, s, c] = ext[c, pl.ds(r, M), :]
-                patch_copy(d, s).start()
+                    stage[d, s, h, c] = wrapped((ext, body)[which], which, c, r, h)
+                patch_copy(d, s, h).start()
+
+    for s in range(min(2, S)):
+        send_patch(s, 1)
+    for d in range(2):
+        @pl.when(row_recv[d])
+        def _():
+            halo_copy(d).wait_recv()
+    for s in range(S):
+        if s >= 2:
+            send_patch(s, 1)
+        send_patch(s, 0)
 
     for step in range(lines + G - 3):
         for there, peer in near_ring:
@@ -240,12 +268,10 @@
         return pltpu.make_async_remote_copy(
             relay.at[h, s], grecv.at[1 - core, h, s], outsem.at[4], gsem.at[1 - core, h], **forward_peer)
 
-    first_half = (grp < G - 1).astype(jnp.int32)
-    halves = [first_half, 1 - first_half]
-
-    for c in locals_[1:3]:
+    for c in locals_[3:6]:
         c.wait()
-    drain(pat, loc.at[3])
+    drain(pat, loc.at[6])
+    drain(prb2, loc.at[7])
     own_count = counts[grp * PN + pos]
 
     column = lax.broadcasted_iota(jnp.int32, (M, M), 1)
@@ -272,32 +298,36 @@
         for d in range(2):
             @pl.when(col_recv[d])
             def _():
-                patch_copy(d, s).wait_recv()
+                drain(nb.at[d, s], patsem.at[d, s])
         back = lax.rem(HALO - shift, HALO)
         forth = lax.rem(shift, HALO)
         first = lane < HALO - shift
         patch = []
         for c in range(2):
-            mid = pltpu.roll(ext[c, pl.ds(r, M), :], back, 1)
-            before = pltpu.roll(nb[1, s, c], back, 1)
-            after = pltpu.roll(nb[0, s, c], back, 1)
+            mid, before, after = [
+                pltpu.roll(stack(*pair), back, 1)
+                for pair in (
+                    [wrapped(ext, 0, c, r, h) for h in range(2)],
+                    [nb[1, s, h, c] for h in range(2)],
+                    [nb[0, s, h, c] for h in range(2)],
+                )
+            ]
             patch.append(side_by_side(jnp.where(first, before, mid), jnp.where(first, mid, after)))
-        pr, pi = prb[0], prb[1]
+        turn = lax.rem(r, M)
+        pr, pi = [side_by_side(*[prb2[c, w, pl.ds(M - turn, M), :] for w in range(2)]) for c in range(2)]
         fr, fi = forward(tab, pr * patch[0] - pi * patch[1], pr * patch[1] + pi * patch[0])
         excess = fr * fr + fi * fi - patp[s]
         excess = jnp.where(jnp.full((M, M), s, jnp.int32) < own_count, excess, 0.0)
         cr, ci = backward(tab, excess * fr, excess * fi)
         parts = (pr * cr + pi * ci, pr * ci - pi * cr)
-        gp[0] += patch[0] * cr + patch[1] * ci
-        gp[1] += patch[0] * ci - patch[1] * cr
+        for c, part in enumerate((patch[0] * cr + patch[1] * ci, patch[0] * ci - patch[1] * cr)):
+            for w in range(2):
+                turned[c, w, :M] = cols_of(part, w)
+                turned[c, w, M:] = cols_of(part, w)
+                gp[c, :, w * HALO : (w + 1) * HALO] += turned[c, w, pl.ds(turn, M), :]
         tail = lane >= shift
         for c in range(2):
-            for w in range(2):
-                turned[c, w, :M] = cols_of(parts[c], w)
-                turned[c, w, M:] = cols_of(parts[c], w)
-        start = M - lax.rem(r, M)
-        for c in range(2):
-            g0, g1 = [pltpu.roll(turned[c, w, pl.ds(start, M), :], forth, 1) for w in range(2)]
+            g0, g1 = [pltpu.roll(cols_of(parts[c], w), forth, 1) for w in range(2)]
             left, middle, right = jnp.where(tail, g0, 0.0), jnp.where(tail, g1, g0), jnp.where(tail, 0.0, g1)
             for h in range(2):
                 gsend[0, h, s, c] = rows_of(left, h)
@@ -558,7 +588,6 @@
     owners, h3 = shares(M, ring)
     f32 = jnp.float32
     V, D = pltpu.VMEM, pltpu.SemaphoreType.DMA
-    smem = pl.BlockSpec(memory_space=pltpu.SMEM)
     hbm = pl.BlockSpec(memory_space=pl.ANY)
     vmem = pl.BlockSpec(memory_space=pltpu.VMEM)
     half = (2, HALO, HALO)
@@ -568,16 +597,20 @@
             pltpu.VMEM(object_field.shape, f32),
             pltpu.VMEM(probe_field.shape, f32),
         ),
-        in_specs=[smem, smem, hbm, hbm, hbm, hbm],
+        in_specs=[hbm] * 6,
         out_specs=(vmem, vmem),
         scratch_shapes=[
+            pltpu.SMEM(corners.shape, jnp.int32),
+            pltpu.SMEM(counts.shape, jnp.int32),
             V((2, TR + 2 * HALO, HALO), f32),
+            V((2, TR, HALO), f32),
             V((2, M, M), f32),
+            V((2, 2, 2 * M, HALO), f32),
             V((2, S, M, HALO), f32),
             V((S, M, M), f32),
             V(tables.shape, jnp.bfloat16),
-            V((2, S, 2, M, HALO), f32),
-            V((2, S, 2, M, HALO), f32),
+            V((2, S, 2, *half), f32),
+            V((2, S, 2, *half), f32),
             pltpu.SMEM((2, *corners.shape), jnp.int32),
             V((S, 2, *half), f32),
             V((2, 2, S, *half), f32),
@@ -592,7 +625,7 @@
             V((2, h3, M), f32),
             V((2, h3, M), f32),
             V((2, M, M), f32),
-            D((4,)), pltpu.SemaphoreType.REGULAR((max(1, grp_size + pos_size // 4 - 3),)), D((2, 2)), D((2, 2)), D((2, S)),
+            D((8,)), pltpu.SemaphoreType.REGULAR((max(1, grp_size + pos_size // 4 - 3),)), D((2, 2)), D((2, 2)), D((2, S)),
             D((2, 2)), D((2,)), D((2, 2)), D((2,)), D((2,)), D((2, ring - 1)), D((2, 2)), D((1,)), D((8,)),
         ],
         compiler_params=pltpu.CompilerParams(

time: 49.5 us -> 49.3 us (level)
  no operation moved by 1% of the time
where the time goes in v5:
time: 49.3 us; the launch traced here: 49.2 us
  Pallas kernels  48.5 us (98%)
  between operations  0.64 us (1%)
    pallas_call x1, Pallas kernels, on_device(): pl.pallas_call(functools.partial(kernel, (grp_size, pos_size, S, TR, M)),...  47.4 us
    pallas_call x1, Pallas kernels, on_device(): pl.pallas_call(store, out_shape=(jax.ShapeDtypeStruct(object_field.shape,...  1.17 us

profile of v5, /device:TPU:0, one launch (start us, length us, event | category | flops | bytes accessed | tf_op | source)
XLA Modules:
  0.0 49.2 jit_solution(7095960262239160030)
XLA Ops:
  0.6 47.4 %shard_map.77 = (f32[2,1024,128]{2,1,0:T(8,128)S(1)}, f32[2,256,256]{2,1,0:T(8,128)S(1)}) custom-call(s32[2,3]{1,0:T(2,128)} %cor_hbm.1, s32[32]{0:T(128)} %cnt_hbm.1, f32[2,1024,128]{2,1,0:T(8,128)} %obj_hbm.1, f32[2,256,256]{2,1,0:T(8,128)} %prb_hbm.1, f32[3,256,256]{2,1,0:T(8,128)} %pat_hbm.1, bf16[2,2,2,256,256]{4,3,2,1,0:T(8,128)(2,1)} %constant.2.clone.tab_hbm), custom_call_target="tpu_custom_call" | custom-call | tf_op jit(solution)/shard_map/pallas_call | solution.py:594
  48.0 1.2 %shard_map.78 = (f32[2,1024,128]{2,1,0:T(8,128)}, f32[2,256,256]{2,1,0:T(8,128)}) custom-call(f32[2,1024,128]{2,1,0:T(8,128)S(1)} %get-tuple-element.4.obj, f32[2,256,256]{2,1,0:T(8,128)S(1)} %get-tuple-element.5.prb), custom_call_target="tpu_custom_call" | custom-call | tf_op jit(solution)/shard_map/pallas_call | solution.py:637

commit v6 on v5

--- a/solution.py
+++ b/solution.py
@@ -11,6 +11,7 @@
 HALO = 128
 STEP_OBJECT = 0.25
 STEP_PROBE = 4.0
+PIECES = 1
 MESH = pl.DeviceIdType.MESH
 
 
@@ -103,7 +104,7 @@
 
 def kernel(sizes, cor_hbm, cnt_hbm, obj_hbm, prb_hbm, pat_hbm, tab_hbm, obj_out, prb_out,
            corners, counts, ext, body, prb, prb2, pat, patp, tab, nb, stage, cor_smem,
-           gmid, gsend, grecv, relay, turned, rim, yrecv, gp, p1r, p3r, p2, p2x, pnew,
+           gmid, gsend, grecv, relay, turned, rim, yrecv, gp, p1r, p3r, p2, p2x,
            loc, farsem, yh, corsem, patsem, gsem, rsem, ysem, csem, asem, agsem, xsem, casem, outsem):
     G, PN, S, TR, M = sizes
     grp, pos = lax.axis_index("grp"), lax.axis_index("pos")
@@ -114,6 +115,7 @@
     me = grp * lines + chip // 2
     late = side != core
     blocks = TR // HALO + 2
+    split_ring = ring == owners and G == 2
 
     def at(g, p):
         return {"device_id": (g, lax.rem(p + PN, PN)), "device_id_type": MESH}
@@ -151,6 +153,7 @@
             locals_.append(pltpu.make_async_copy(
                 prb_hbm.at[:, :, columns], prb2.at[:, w, pl.ds(turn * M, M), :], loc.at[7]))
 
+    locals_[0].start()
     near_ring = [
         (late & row_send[0], row_peer[0]), (late & row_send[1], row_peer[1]),
         (late & (pos >= 4), at(grp, pos - 4)), (late & (pos + 4 < PN), at(grp, pos + 4)),
@@ -169,13 +172,12 @@
     expected += greet(near_ring[2][0], [near_ring[2][1]]) + greet(near_ring[3][0], [near_ring[3][1]])
     expected += greet(~late & has_outer, [relay_peer, feeder]) + greet(has_relay, [relay_peer, forward_peer])
 
-    for c in locals_:
+    for c in locals_[1:3]:
         c.start()
     lane = lax.broadcasted_iota(jnp.int32, (M, HALO), 1)
     gp[...] = jnp.zeros(gp.shape, jnp.float32)
 
-    for c in locals_[:3]:
-        c.wait()
+    locals_[0].wait()
     pl.semaphore_wait(barrier, expected)
 
     def cor_copy(d):
@@ -193,7 +195,11 @@
         @pl.when(col_send[d])
         def _():
             cor_copy(d).start()
-
+    for c in locals_[1:3]:
+        c.wait()
+    for c in locals_[3:]:
+        c.start()
+    for d in range(2):
         @pl.when(row_send[d])
         def _():
             halo_copy(d).start()
@@ -356,18 +362,40 @@
         return pltpu.make_async_remote_copy(
             gp.at[c, share_rows(ring_at(k)), :], p3r.at[c, k - 1], outsem.at[5], asem.at[c], **ring_peer(k))
 
+    line = chip // 2
+
+    def line_at(k):
+        return lax.rem(line + k + lines, lines)
+
+    def line_peer(k):
+        return at(grp, (line_at(k) * 2 + side) * 2 + core)
+
+    def group_at(j):
+        return lax.rem(grp + j + G, G)
+
+    def line_spread(c, k, owner):
+        rows = share_rows(owner)
+        return pltpu.make_async_remote_copy(
+            prb_out.at[c, rows, :], prb_out.at[c, rows, :], outsem.at[6 + c], agsem.at[c, k - 1], **line_peer(k))
+
+    def group_spread(c, j, k, owner):
+        rows = share_rows(owner)
+        return pltpu.make_async_remote_copy(
+            prb_out.at[c, rows, :], prb_out.at[c, rows, :], outsem.at[8 + c], agsem.at[c, lines - 1 + (j - 1) * lines + k],
+            **at(group_at(j), pos))
+
     def across_copy(c):
         return pltpu.make_async_remote_copy(p2.at[c], p2x.at[c], xsem.at[0, c], xsem.at[1, c], **across)
 
     def spread_copy(c, k, owner):
         rows = share_rows(owner)
         return pltpu.make_async_remote_copy(
-            pnew.at[c, rows, :], pnew.at[c, rows, :], outsem.at[6], agsem.at[c, k - 1], **ring_peer(k))
+            prb_out.at[c, rows, :], prb_out.at[c, rows, :], outsem.at[6], agsem.at[c, k - 1], **ring_peer(k))
 
     def hand_copy(c, owner):
         rows = share_rows(owner)
         return pltpu.make_async_remote_copy(
-            pnew.at[c, rows, :], pnew.at[c, rows, :], outsem.at[7], casem.at[0], **partner)
+            prb_out.at[c, rows, :], prb_out.at[c, rows, :], outsem.at[10], casem.at[0], **partner)
 
     def source(k):
         return lax.rem(me + ring - k, ring)
@@ -435,7 +463,6 @@
                 @pl.when(ring_at(k) < owners)
                 def _():
                     share_copy(c, k).start()
-
         pass_on(halves[0])
         near_all()
         for c in range(2):
@@ -461,9 +488,14 @@
                 across_copy(c).wait_recv()
                 total = p2[c] + p2x[c]
                 divisor = jnp.full(total.shape, live, jnp.int32).astype(jnp.float32)
-                pnew[c, share_rows(me), :] = prb[c, share_rows(me), :] - STEP_PROBE * total / divisor
-                for k in range(1, ring):
-                    spread_copy(c, k, me).start()
+                prb_out[c, share_rows(me), :] = prb[c, share_rows(me), :] - STEP_PROBE * total / divisor
+                if split_ring:
+                    for k in range(1, lines):
+                        line_spread(c, k, me).start()
+                    group_spread(c, 1, 0, me).start()
+                else:
+                    for k in range(1, ring):
+                        spread_copy(c, k, me).start()
                 hand_copy(c, me).start()
 
     def rim_copy(d):
@@ -502,17 +534,30 @@
             lax.fori_loop(0, blocks // 2 - 1, far, 0)
 
     finish(halves[0])
+    finish(halves[1])
 
     @pl.when(late)
     def _():
-        for c in range(2):
-            for k in range(1, ring):
-                @pl.when(source(k) < owners)
-                def _():
-                    spread_copy(c, k, source(k)).wait_recv()
-                    hand_copy(c, source(k)).start()
-
-    finish(halves[1])
+        if split_ring:
+            for c in range(2):
+                for k in range(1, lines):
+                    owner = grp * lines + line_at(-k)
+                    line_spread(c, k, owner).wait_recv()
+                    group_spread(c, 1, k, owner).start()
+                    hand_copy(c, owner).start()
+            for c in range(2):
+                for k in range(lines):
+                    owner = group_at(1) * lines + line_at(-k)
+                    group_spread(c, 1, k, owner).wait_recv()
+                    hand_copy(c, owner).start()
+        else:
+            for c in range(2):
+                for k in range(1, ring):
+                    @pl.when(source(k) < owners)
+                    def _():
+                        spread_copy(c, k, source(k)).wait_recv()
+                        hand_copy(c, source(k)).start()
+
     for d in range(2):
         @pl.when(row_recv[d])
         def _():
@@ -522,8 +567,7 @@
 
     @pl.when(~late)
     def _():
-        drain(pnew, casem.at[0])
-    prb_out[...] = pnew[...]
+        drain(prb_out, casem.at[0])
 
     for d in range(2):
         @pl.when(col_send[d])
@@ -551,9 +595,11 @@
 
     @pl.when(late)
     def _():
-        if ring == owners:
+        if split_ring:
             drain(p3r, outsem.at[5])
-            drain(p3r, outsem.at[6])
+            for c in range(2):
+                drain(prb_out.at[c, pl.ds(0, (lines - 1) * h3), :], outsem.at[6 + c])
+                drain(prb_out.at[c, pl.ds(0, (G - 1) * lines * h3), :], outsem.at[8 + c])
         else:
             for c in range(2):
                 for k in range(1, ring):
@@ -570,12 +616,15 @@
         def _():
             for c in range(2):
                 across_copy(c).wait_send()
-        drain(pnew, outsem.at[7])
+        drain(prb_out, outsem.at[10])
 
 
 def store(obj, prb, obj_out, prb_out, sems):
-    copies = [pltpu.make_async_copy(obj.at[c], obj_out.at[c], sems.at[c]) for c in range(2)]
-    copies.append(pltpu.make_async_copy(prb, prb_out, sems.at[2]))
+    pairs = []
+    for whole, out in ((obj, obj_out), (prb, prb_out)):
+        rows = whole.shape[1] // PIECES
+        pairs += [(whole.at[:, pl.ds(i * rows, rows), :], out.at[:, pl.ds(i * rows, rows), :]) for i in range(PIECES)]
+    copies = [pltpu.make_async_copy(*pair, sems.at[i]) for i, pair in enumerate(pairs)]
     for c in copies:
         c.start()
     for c in copies:
@@ -624,9 +673,8 @@
             V((2, ring - 1, h3, M), f32),
             V((2, h3, M), f32),
             V((2, h3, M), f32),
-            V((2, M, M), f32),
             D((8,)), pltpu.SemaphoreType.REGULAR((max(1, grp_size + pos_size // 4 - 3),)), D((2, 2)), D((2, 2)), D((2, S)),
-            D((2, 2)), D((2,)), D((2, 2)), D((2,)), D((2,)), D((2, ring - 1)), D((2, 2)), D((1,)), D((8,)),
+            D((2, 2)), D((2,)), D((2, 2)), D((2,)), D((2,)), D((2, ring - 1)), D((2, 2)), D((1,)), D((11,)),
         ],
         compiler_params=pltpu.CompilerParams(
             collective_id=0, has_side_effects=True, vmem_limit_bytes=56 * 1024 * 1024
@@ -642,7 +690,7 @@
         ),
         in_specs=[hbm, hbm],
         out_specs=(hbm, hbm),
-        scratch_shapes=[D((3,))],
+        scratch_shapes=[D((2 * PIECES,))],
         compiler_params=pltpu.CompilerParams(vmem_limit_bytes=1024 * 1024),
     )(object_new, probe_new)
 

time: 49.3 us -> 48.5 us (0.984)
  Pallas kernels: 48.5 us -> 47.7 us
    pallas_call x1, Pallas kernels: 47.4 us -> 46.6 us  [on_device(): pl.pallas_call(functools.partial(kernel, (grp_size, pos_size, S, TR, M)),...]
where the time goes in v6:
time: 48.5 us; the launch traced here: 48.4 us
  Pallas kernels  47.7 us (98%)
  between operations  0.64 us (1%)
    pallas_call x1, Pallas kernels, on_device(): pl.pallas_call(functools.partial(kernel, (grp_size, pos_size, S, TR, M)),...  46.6 us
    pallas_call x1, Pallas kernels, on_device(): pl.pallas_call(store, out_shape=(jax.ShapeDtypeStruct(object_field.shape,...  1.16 us

profile of v6, /device:TPU:0, one launch (start us, length us, event | category | flops | bytes accessed | tf_op | source)
XLA Modules:
  0.0 48.4 jit_solution(5732633891010882227)
XLA Ops:
  0.6 46.6 %shard_map.77 = (f32[2,1024,128]{2,1,0:T(8,128)S(1)}, f32[2,256,256]{2,1,0:T(8,128)S(1)}) custom-call(s32[2,3]{1,0:T(2,128)} %cor_hbm.1, s32[32]{0:T(128)} %cnt_hbm.1, f32[2,1024,128]{2,1,0:T(8,128)} %obj_hbm.1, f32[2,256,256]{2,1,0:T(8,128)} %prb_hbm.1, f32[3,256,256]{2,1,0:T(8,128)} %pat_hbm.1, bf16[2,2,2,256,256]{4,3,2,1,0:T(8,128)(2,1)} %constant.2.clone.tab_hbm), custom_call_target="tpu_custom_call" | custom-call | tf_op jit(solution)/shard_map/pallas_call | solution.py:643
  47.2 1.2 %shard_map.78 = (f32[2,1024,128]{2,1,0:T(8,128)}, f32[2,256,256]{2,1,0:T(8,128)}) custom-call(f32[2,1024,128]{2,1,0:T(8,128)S(1)} %get-tuple-element.4.obj, f32[2,256,256]{2,1,0:T(8,128)S(1)} %get-tuple-element.5.prb), custom_call_target="tpu_custom_call" | custom-call | tf_op jit(solution)/shard_map/pallas_call | solution.py:685

commit v7 on v6

--- a/solution.py
+++ b/solution.py
@@ -358,9 +358,18 @@
     def share_rows(q):
         return pl.ds(pl.multiple_of(lax.rem(q, owners) * h3, 8), h3)
 
-    def share_copy(c, k):
+    pieces = M // HALO
+
+    def chunk(q, owner):
+        return q // pieces, share_rows(owner), pl.ds(q % pieces * HALO, HALO)
+
+    def share_copy(q, k):
         return pltpu.make_async_remote_copy(
-            gp.at[c, share_rows(ring_at(k)), :], p3r.at[c, k - 1], outsem.at[5], asem.at[c], **ring_peer(k))
+            gp.at[chunk(q, ring_at(k))], p3r.at[q, k - 1], outsem.at[5], asem.at[q], **ring_peer(k))
+
+    def pass_share(q, owner, send_sem, recv_sem, peer):
+        where = chunk(q, owner)
+        return pltpu.make_async_remote_copy(prb_out.at[where], prb_out.at[where], send_sem, recv_sem, **peer)
 
     line = chip // 2
 
@@ -373,29 +382,22 @@
     def group_at(j):
         return lax.rem(grp + j + G, G)
 
-    def line_spread(c, k, owner):
-        rows = share_rows(owner)
-        return pltpu.make_async_remote_copy(
-            prb_out.at[c, rows, :], prb_out.at[c, rows, :], outsem.at[6 + c], agsem.at[c, k - 1], **line_peer(k))
-
-    def group_spread(c, j, k, owner):
-        rows = share_rows(owner)
-        return pltpu.make_async_remote_copy(
-            prb_out.at[c, rows, :], prb_out.at[c, rows, :], outsem.at[8 + c], agsem.at[c, lines - 1 + (j - 1) * lines + k],
-            **at(group_at(j), pos))
-
-    def across_copy(c):
-        return pltpu.make_async_remote_copy(p2.at[c], p2x.at[c], xsem.at[0, c], xsem.at[1, c], **across)
-
-    def spread_copy(c, k, owner):
-        rows = share_rows(owner)
-        return pltpu.make_async_remote_copy(
-            prb_out.at[c, rows, :], prb_out.at[c, rows, :], outsem.at[6], agsem.at[c, k - 1], **ring_peer(k))
-
-    def hand_copy(c, owner):
-        rows = share_rows(owner)
-        return pltpu.make_async_remote_copy(
-            prb_out.at[c, rows, :], prb_out.at[c, rows, :], outsem.at[10], casem.at[0], **partner)
+    def line_spread(q, k):
+        return pass_share(q, me, outsem.at[6], agsem.at[q, 0], line_peer(k))
+
+    def group_spread(q, owner):
+        return pass_share(q, owner, outsem.at[7], agsem.at[q, 1], at(group_at(1), pos))
+
+    def spread_copy(q, k, owner):
+        return pass_share(q, owner, outsem.at[6], agsem.at[q, 0], ring_peer(k))
+
+    def hand_copy(q, owner):
+        return pass_share(q, owner, outsem.at[8], casem.at[0], partner)
+
+    def across_copy(q):
+        return pltpu.make_async_remote_copy(p2.at[q], p2x.at[q], xsem.at[0, q], xsem.at[1, q], **across)
+
+    chunks = range(2 * pieces)
 
     def source(k):
         return lax.rem(me + ring - k, ring)
@@ -458,24 +460,26 @@
     def _():
         core_copy.wait_recv()
         gp[...] += p1r[...]
-        for c in range(2):
+        for q in chunks:
             for k in range(1, ring):
                 @pl.when(ring_at(k) < owners)
                 def _():
-                    share_copy(c, k).start()
+                    share_copy(q, k).start()
         pass_on(halves[0])
         near_all()
-        for c in range(2):
+        for q in chunks:
             @pl.when(me < owners)
             def _():
-                total = gp[c, share_rows(me), :]
-                drain(p3r.at[c], asem.at[c])
+                total = gp[chunk(q, me)]
+                drain(p3r.at[q], asem.at[q])
                 for k in range(ring - 1):
-                    total = total + p3r[c, k]
-                p2[c] = total
-                across_copy(c).start()
-
-            second(*((0, 1), (1, S))[c])
+                    total = total + p3r[q, k]
+                p2[q] = total
+                across_copy(q).start()
+
+            if q == pieces - 1:
+                second(0, 1)
+        second(1, S)
 
         pass_on(halves[1])
         live = counts[0]
@@ -484,19 +488,19 @@
 
         @pl.when(me < owners)
         def _():
-            for c in range(2):
-                across_copy(c).wait_recv()
-                total = p2[c] + p2x[c]
+            for q in chunks:
+                across_copy(q).wait_recv()
+                total = p2[q] + p2x[q]
                 divisor = jnp.full(total.shape, live, jnp.int32).astype(jnp.float32)
-                prb_out[c, share_rows(me), :] = prb[c, share_rows(me), :] - STEP_PROBE * total / divisor
+                prb_out[chunk(q, me)] = prb[chunk(q, me)] - STEP_PROBE * total / divisor
                 if split_ring:
                     for k in range(1, lines):
-                        line_spread(c, k, me).start()
-                    group_spread(c, 1, 0, me).start()
+                        line_spread(q, k).start()
+                    group_spread(q, me).start()
                 else:
                     for k in range(1, ring):
-                        spread_copy(c, k, me).start()
-                hand_copy(c, me).start()
+                        spread_copy(q, k, me).start()
+                hand_copy(q, me).start()
 
     def rim_copy(d):
         return pltpu.make_async_remote_copy(rim.at[d], yrecv.at[d], ysem.at[0, d], ysem.at[1, d], **row_peer[d])
@@ -539,24 +543,23 @@
     @pl.when(late)
     def _():
         if split_ring:
-            for c in range(2):
+            for q in chunks:
+                drain(prb_out.at[0, pl.ds(0, (lines - 1) * h3), pl.ds(0, HALO)], agsem.at[q, 0])
                 for k in range(1, lines):
                     owner = grp * lines + line_at(-k)
-                    line_spread(c, k, owner).wait_recv()
-                    group_spread(c, 1, k, owner).start()
-                    hand_copy(c, owner).start()
-            for c in range(2):
+                    group_spread(q, owner).start()
+                    hand_copy(q, owner).start()
+            for q in chunks:
+                drain(prb_out.at[0, pl.ds(0, lines * h3), pl.ds(0, HALO)], agsem.at[q, 1])
                 for k in range(lines):
-                    owner = group_at(1) * lines + line_at(-k)
-                    group_spread(c, 1, k, owner).wait_recv()
-                    hand_copy(c, owner).start()
+                    hand_copy(q, group_at(1) * lines + line_at(-k)).start()
         else:
-            for c in range(2):
+            for q in chunks:
                 for k in range(1, ring):
                     @pl.when(source(k) < owners)
                     def _():
-                        spread_copy(c, k, source(k)).wait_recv()
-                        hand_copy(c, source(k)).start()
+                        spread_copy(q, k, source(k)).wait_recv()
+                        hand_copy(q, source(k)).start()
 
     for d in range(2):
         @pl.when(row_recv[d])
@@ -597,26 +600,25 @@
     def _():
         if split_ring:
             drain(p3r, outsem.at[5])
-            for c in range(2):
-                drain(prb_out.at[c, pl.ds(0, (lines - 1) * h3), :], outsem.at[6 + c])
-                drain(prb_out.at[c, pl.ds(0, (G - 1) * lines * h3), :], outsem.at[8 + c])
+            drain(prb_out.at[:, pl.ds(0, (lines - 1) * h3), :], outsem.at[6])
+            drain(prb_out.at[:, pl.ds(0, lines * h3), :], outsem.at[7])
         else:
-            for c in range(2):
+            for q in chunks:
                 for k in range(1, ring):
                     @pl.when(ring_at(k) < owners)
                     def _():
-                        share_copy(c, k).wait_send()
+                        share_copy(q, k).wait_send()
 
                 @pl.when(me < owners)
                 def _():
                     for k in range(1, ring):
-                        spread_copy(c, k, me).wait_send()
+                        spread_copy(q, k, me).wait_send()
 
         @pl.when(me < owners)
         def _():
-            for c in range(2):
-                across_copy(c).wait_send()
-        drain(prb_out, outsem.at[10])
+            for q in chunks:
+                across_copy(q).wait_send()
+        drain(prb_out, outsem.at[8])
 
 
 def store(obj, prb, obj_out, prb_out, sems):
@@ -639,7 +641,7 @@
     V, D = pltpu.VMEM, pltpu.SemaphoreType.DMA
     hbm = pl.BlockSpec(memory_space=pl.ANY)
     vmem = pl.BlockSpec(memory_space=pltpu.VMEM)
-    half = (2, HALO, HALO)
+    half, chunks = (2, HALO, HALO), 2 * (M // HALO)
     object_new, probe_new = pl.pallas_call(
         functools.partial(kernel, (grp_size, pos_size, S, TR, M)),
         out_shape=(
@@ -670,11 +672,11 @@
             V((2, *half), f32),
             V((2, M, M), f32),
             V((2, M, M), f32),
-            V((2, ring - 1, h3, M), f32),
-            V((2, h3, M), f32),
-            V((2, h3, M), f32),
+            V((chunks, ring - 1, h3, HALO), f32),
+            V((chunks, h3, HALO), f32),
+            V((chunks, h3, HALO), f32),
             D((8,)), pltpu.SemaphoreType.REGULAR((max(1, grp_size + pos_size // 4 - 3),)), D((2, 2)), D((2, 2)), D((2, S)),
-            D((2, 2)), D((2,)), D((2, 2)), D((2,)), D((2,)), D((2, ring - 1)), D((2, 2)), D((1,)), D((11,)),
+            D((2, 2)), D((2,)), D((2, 2)), D((2,)), D((chunks,)), D((chunks, 2)), D((2, chunks)), D((1,)), D((9,)),
         ],
         compiler_params=pltpu.CompilerParams(
             collective_id=0, has_side_effects=True, vmem_limit_bytes=56 * 1024 * 1024

time: 48.5 us -> 48 us (0.990)
  Pallas kernels: 47.7 us -> 47.2 us
    pallas_call x1, Pallas kernels: 46.6 us -> 46.1 us  [on_device(): pl.pallas_call(functools.partial(kernel, (grp_size, pos_size, S, TR, M)),...]
where the time goes in v7:
time: 48 us; the launch traced here: 47.9 us
  Pallas kernels  47.2 us (98%)
  between operations  0.64 us (1%)
    pallas_call x1, Pallas kernels, on_device(): pl.pallas_call(functools.partial(kernel, (grp_size, pos_size, S, TR, M)),...  46.1 us
    pallas_call x1, Pallas kernels, on_device(): pl.pallas_call(store, out_shape=(jax.ShapeDtypeStruct(object_field.shape,...  1.16 us

profile of v7, /device:TPU:0, one launch (start us, length us, event | category | flops | bytes accessed | tf_op | source)
XLA Modules:
  0.0 47.9 jit_solution(4255856662661556560)
XLA Ops:
  0.6 46.1 %shard_map.77 = (f32[2,1024,128]{2,1,0:T(8,128)S(1)}, f32[2,256,256]{2,1,0:T(8,128)S(1)}) custom-call(s32[2,3]{1,0:T(2,128)} %cor_hbm.1, s32[32]{0:T(128)} %cnt_hbm.1, f32[2,1024,128]{2,1,0:T(8,128)} %obj_hbm.1, f32[2,256,256]{2,1,0:T(8,128)} %prb_hbm.1, f32[3,256,256]{2,1,0:T(8,128)} %pat_hbm.1, bf16[2,2,2,256,256]{4,3,2,1,0:T(8,128)(2,1)} %constant.2.clone.tab_hbm), custom_call_target="tpu_custom_call" | custom-call | tf_op jit(solution)/shard_map/pallas_call | solution.py:645
  46.7 1.2 %shard_map.78 = (f32[2,1024,128]{2,1,0:T(8,128)}, f32[2,256,256]{2,1,0:T(8,128)}) custom-call(f32[2,1024,128]{2,1,0:T(8,128)S(1)} %get-tuple-element.4.obj, f32[2,256,256]{2,1,0:T(8,128)S(1)} %get-tuple-element.5.prb), custom_call_target="tpu_custom_call" | custom-call | tf_op jit(solution)/shard_map/pallas_call | solution.py:687

commit v8 on v7

--- a/solution.py
+++ b/solution.py
@@ -104,8 +104,8 @@
 
 def kernel(sizes, cor_hbm, cnt_hbm, obj_hbm, prb_hbm, pat_hbm, tab_hbm, obj_out, prb_out,
            corners, counts, ext, body, prb, prb2, pat, patp, tab, nb, stage, cor_smem,
-           gmid, gsend, grecv, relay, turned, rim, yrecv, gp, p1r, p3r, p2, p2x,
-           loc, farsem, yh, corsem, patsem, gsem, rsem, ysem, csem, asem, agsem, xsem, casem, outsem):
+           gmid, gsend, grecv, relay, turned, rim, yrecv, gp, p1r, p3r, gpr, p2, p2x,
+           loc, farsem, yh, corsem, patsem, gsem, rsem, ysem, csem, asem, agsem, xsem, casem, gprsem, outsem):
     G, PN, S, TR, M = sizes
     grp, pos = lax.axis_index("grp"), lax.axis_index("pos")
     core, chip, chips = lax.rem(pos, 2), pos // 2, PN // 2
@@ -367,6 +367,17 @@
         return pltpu.make_async_remote_copy(
             gp.at[chunk(q, ring_at(k))], p3r.at[q, k - 1], outsem.at[5], asem.at[q], **ring_peer(k))
 
+    group_rows = pl.ds(pl.multiple_of(grp * lines * h3, 8), lines * h3)
+
+    def group_share():
+        other = group_at(1)
+        rows = pl.ds(pl.multiple_of(other * lines * h3, 8), lines * h3)
+        return pltpu.make_async_remote_copy(gp.at[1, rows, :], gpr, outsem.at[10], gprsem.at[0], **at(other, pos))
+
+    def line_share(q, k):
+        return pltpu.make_async_remote_copy(
+            gp.at[chunk(q, grp * lines + line_at(k))], p3r.at[q, k - 1], outsem.at[11], asem.at[q], **line_peer(k))
+
     def pass_share(q, owner, send_sem, recv_sem, peer):
         where = chunk(q, owner)
         return pltpu.make_async_remote_copy(prb_out.at[where], prb_out.at[where], send_sem, recv_sem, **peer)
@@ -395,9 +406,10 @@
         return pass_share(q, owner, outsem.at[8], casem.at[0], partner)
 
     def across_copy(q):
-        return pltpu.make_async_remote_copy(p2.at[q], p2x.at[q], xsem.at[0, q], xsem.at[1, q], **across)
+        return pltpu.make_async_remote_copy(p2.at[q], p2x.at[q], outsem.at[9], xsem.at[q], **across)
 
     chunks = range(2 * pieces)
+    direct = chunks[:pieces] if split_ring else chunks
 
     def source(k):
         return lax.rem(me + ring - k, ring)
@@ -460,19 +472,28 @@
     def _():
         core_copy.wait_recv()
         gp[...] += p1r[...]
-        for q in chunks:
+        if split_ring:
+            group_share().start()
+        for q in direct:
             for k in range(1, ring):
                 @pl.when(ring_at(k) < owners)
                 def _():
                     share_copy(q, k).start()
         pass_on(halves[0])
         near_all()
+        if split_ring:
+            drain(gpr, gprsem.at[0])
+            gp[1, group_rows, :] += gpr[...]
+            for q in chunks[pieces:]:
+                for k in range(1, lines):
+                    line_share(q, k).start()
         for q in chunks:
             @pl.when(me < owners)
             def _():
                 total = gp[chunk(q, me)]
-                drain(p3r.at[q], asem.at[q])
-                for k in range(ring - 1):
+                terms = (ring if q in direct else lines) - 1
+                drain(p3r.at[q, pl.ds(0, terms)], asem.at[q])
+                for k in range(terms):
                     total = total + p3r[q, k]
                 p2[q] = total
                 across_copy(q).start()
@@ -538,7 +559,6 @@
             lax.fori_loop(0, blocks // 2 - 1, far, 0)
 
     finish(halves[0])
-    finish(halves[1])
 
     @pl.when(late)
     def _():
@@ -549,10 +569,6 @@
                     owner = grp * lines + line_at(-k)
                     group_spread(q, owner).start()
                     hand_copy(q, owner).start()
-            for q in chunks:
-                drain(prb_out.at[0, pl.ds(0, lines * h3), pl.ds(0, HALO)], agsem.at[q, 1])
-                for k in range(lines):
-                    hand_copy(q, group_at(1) * lines + line_at(-k)).start()
         else:
             for q in chunks:
                 for k in range(1, ring):
@@ -561,6 +577,16 @@
                         spread_copy(q, k, source(k)).wait_recv()
                         hand_copy(q, source(k)).start()
 
+    if split_ring:
+        @pl.when(late)
+        def _():
+            for q in chunks:
+                drain(prb_out.at[0, pl.ds(0, lines * h3), pl.ds(0, HALO)], agsem.at[q, 1])
+                for k in range(lines):
+                    hand_copy(q, group_at(1) * lines + line_at(-k)).start()
+
+    finish(halves[1])
+
     for d in range(2):
         @pl.when(row_recv[d])
         def _():
@@ -599,7 +625,9 @@
     @pl.when(late)
     def _():
         if split_ring:
-            drain(p3r, outsem.at[5])
+            drain(p3r.at[pl.ds(0, pieces)], outsem.at[5])
+            drain(gpr, outsem.at[10])
+            drain(p3r.at[pl.ds(pieces, pieces), pl.ds(0, lines - 1)], outsem.at[11])
             drain(prb_out.at[:, pl.ds(0, (lines - 1) * h3), :], outsem.at[6])
             drain(prb_out.at[:, pl.ds(0, lines * h3), :], outsem.at[7])
         else:
@@ -616,8 +644,7 @@
 
         @pl.when(me < owners)
         def _():
-            for q in chunks:
-                across_copy(q).wait_send()
+            drain(p2, outsem.at[9])
         drain(prb_out, outsem.at[8])
 
 
@@ -673,10 +700,11 @@
             V((2, M, M), f32),
             V((2, M, M), f32),
             V((chunks, ring - 1, h3, HALO), f32),
+            V((M // grp_size, M), f32),
             V((chunks, h3, HALO), f32),
             V((chunks, h3, HALO), f32),
             D((8,)), pltpu.SemaphoreType.REGULAR((max(1, grp_size + pos_size // 4 - 3),)), D((2, 2)), D((2, 2)), D((2, S)),
-            D((2, 2)), D((2,)), D((2, 2)), D((2,)), D((chunks,)), D((chunks, 2)), D((2, chunks)), D((1,)), D((9,)),
+            D((2, 2)), D((2,)), D((2, 2)), D((2,)), D((chunks,)), D((chunks, 2)), D((chunks,)), D((1,)), D((1,)), D((12,)),
         ],
         compiler_params=pltpu.CompilerParams(
             collective_id=0, has_side_effects=True, vmem_limit_bytes=56 * 1024 * 1024

time: 48 us -> 47.7 us (level)
  Pallas kernels: 47.2 us -> 46.7 us
    pallas_call x1, Pallas kernels: 46.1 us -> 45.5 us  [on_device(): pl.pallas_call(functools.partial(kernel, (grp_size, pos_size, S, TR, M)),...]
where the time goes in v8:
time: 47.7 us; the launch traced here: 47.3 us
  Pallas kernels  46.7 us (98%)
  between operations  0.64 us (1%)
    pallas_call x1, Pallas kernels, on_device(): pl.pallas_call(functools.partial(kernel, (grp_size, pos_size, S, TR, M)),...  45.5 us
    pallas_call x1, Pallas kernels, on_device(): pl.pallas_call(store, out_shape=(jax.ShapeDtypeStruct(object_field.shape,...  1.16 us

profile of v8, /device:TPU:0, one launch (start us, length us, event | category | flops | bytes accessed | tf_op | source)
XLA Modules:
  0.0 47.3 jit_solution(7293156036513474941)
XLA Ops:
  0.6 45.5 %shard_map.77 = (f32[2,1024,128]{2,1,0:T(8,128)S(1)}, f32[2,256,256]{2,1,0:T(8,128)S(1)}) custom-call(s32[2,3]{1,0:T(2,128)} %cor_hbm.1, s32[32]{0:T(128)} %cnt_hbm.1, f32[2,1024,128]{2,1,0:T(8,128)} %obj_hbm.1, f32[2,256,256]{2,1,0:T(8,128)} %prb_hbm.1, f32[3,256,256]{2,1,0:T(8,128)} %pat_hbm.1, bf16[2,2,2,256,256]{4,3,2,1,0:T(8,128)(2,1)} %constant.2.clone.tab_hbm), custom_call_target="tpu_custom_call" | custom-call | tf_op jit(solution)/shard_map/pallas_call | solution.py:672
  46.2 1.2 %shard_map.78 = (f32[2,1024,128]{2,1,0:T(8,128)}, f32[2,256,256]{2,1,0:T(8,128)}) custom-call(f32[2,1024,128]{2,1,0:T(8,128)S(1)} %get-tuple-element.4.obj, f32[2,256,256]{2,1,0:T(8,128)S(1)} %get-tuple-element.5.prb), custom_call_target="tpu_custom_call" | custom-call | tf_op jit(solution)/shard_map/pallas_call | solution.py:715

commit v9 on v8

--- a/solution.py
+++ b/solution.py
@@ -471,9 +471,10 @@
     @pl.when(late)
     def _():
         core_copy.wait_recv()
-        gp[...] += p1r[...]
+        gp[1] += p1r[1]
         if split_ring:
             group_share().start()
+        gp[0] += p1r[0]
         for q in direct:
             for k in range(1, ring):
                 @pl.when(ring_at(k) < owners)

time: 47.7 us -> 47.9 us (level)
  no operation moved by 1% of the time
where the time goes in v9:
time: 47.9 us; the launch traced here: 47.7 us
  Pallas kernels  47 us (98%)
  between operations  0.64 us (1%)
    pallas_call x1, Pallas kernels, on_device(): pl.pallas_call(functools.partial(kernel, (grp_size, pos_size, S, TR, M)),...  45.9 us
    pallas_call x1, Pallas kernels, on_device(): pl.pallas_call(store, out_shape=(jax.ShapeDtypeStruct(object_field.shape,...  1.16 us

profile of v9, /device:TPU:0, one launch (start us, length us, event | category | flops | bytes accessed | tf_op | source)
XLA Modules:
  0.0 47.7 jit_solution(7254296822236287426)
XLA Ops:
  0.6 45.9 %shard_map.77 = (f32[2,1024,128]{2,1,0:T(8,128)S(1)}, f32[2,256,256]{2,1,0:T(8,128)S(1)}) custom-call(s32[2,3]{1,0:T(2,128)} %cor_hbm.1, s32[32]{0:T(128)} %cnt_hbm.1, f32[2,1024,128]{2,1,0:T(8,128)} %obj_hbm.1, f32[2,256,256]{2,1,0:T(8,128)} %prb_hbm.1, f32[3,256,256]{2,1,0:T(8,128)} %pat_hbm.1, bf16[2,2,2,256,256]{4,3,2,1,0:T(8,128)(2,1)} %constant.2.clone.tab_hbm), custom_call_target="tpu_custom_call" | custom-call | tf_op jit(solution)/shard_map/pallas_call | solution.py:673
  46.5 1.2 %shard_map.78 = (f32[2,1024,128]{2,1,0:T(8,128)}, f32[2,256,256]{2,1,0:T(8,128)}) custom-call(f32[2,1024,128]{2,1,0:T(8,128)S(1)} %get-tuple-element.4.obj, f32[2,256,256]{2,1,0:T(8,128)S(1)} %get-tuple-element.5.prb), custom_call_target="tpu_custom_call" | custom-call | tf_op jit(solution)/shard_map/pallas_call | solution.py:716
